TPU v7x, 512 devices: a whole 4x8x8 slice. The times are simulated.
512 devices in a mesh: ka: 16 (over x_hi, y), mode: 8 (over z), row: 4 (over x_lo, core).
Axes of the slice: x: 4 (x_hi: 2, x_lo: 2; x = x_hi * 2 + x_lo), y: 8, z: 8, core: 2. Of those that a mesh axis runs over, the one named last changes fastest.
Arguments:
- vectors: float32 [16, 8, 16, 16, 8, 512], P('ka', None, 'mode', 'row'), may hold values from -6 to 6
- previous: float32 [16, 8, 16, 16, 8, 512], P('ka', None, 'mode', 'row'), may hold values from -6 to 6
- beta: float32 [8, 8], replicated, may hold values from -2 to 2
- potential: float32 [16, 16, 8, 512], P('mode', 'row'), may hold values from 0.1 to 10
- coriolis_fn: float32 [16, 16, 8, 512], P('mode', 'row'), may hold values from 0.5 to 2
- second_fn: float32 [16, 16, 8, 512], P('mode', 'row'), may hold values from 0.5 to 2
- rot_const: float32 [16], replicated, may hold values from 0.02 to 0.06
- coupling: float32 [2, 16], replicated, may hold values from 0.3 to 1.5
- kin_one: float32 [16, 16], replicated, may hold values from -1.5 to 1.5
- kin_two: float32 [16, 16], replicated, may hold values from -1.5 to 1.5
- kin_three: float32 [8, 8], replicated, may hold values from -2 to 2
- kin_four: float32 [8, 8], replicated, may hold values from -2 to 2
- kin_five: float32 [8, 8], replicated, may hold values from -2 to 2
- kin_six: float32 [8, 8], replicated, may hold values from -2 to 2
- coriolis_derivative: float32 [8, 8], replicated, may hold values from -2 to 2
Outputs:
- basis: float32 [16, 8, 16, 16, 8, 512], P('ka', None, 'mode', 'row')
- alpha: float32 [8, 8], replicated
- lower_factor: float32 [8, 8], replicated
All inputs are finite; a program needn't handle non-finite values.
Results may differ from a plain program's by a relative error of at most 0.0003.
Values sent between devices are 32-bit elements; how exact they have to be, the bound alone decides.
A program may use at most 128 MiB of HBM per device.

v0:
```python
import jax
import jax.numpy as jnp
from jax import lax
from jax.sharding import PartitionSpec as P

precise_mode = lax.Precision.HIGHEST


def passed_along(value, axis, by):
    peers = lax.axis_size(axis)
    pairs = [(i, i + by) for i in range(peers) if 0 <= i + by < peers]
    return lax.ppermute(value, axis, pairs)


def symmetric(matrix):
    return 0.5 * (matrix + matrix.T)


def along_first(matrix, field):
    return jnp.einsum("ab,nbyz->nayz", matrix, field, precision=precise_mode)


def along_second(matrix, field):
    return jnp.einsum("ab,nxbz->nxaz", matrix, field, precision=precise_mode)


def along_third(matrix, field):
    return jnp.einsum("ab,nxybz->nxyaz", matrix, field, precision=precise_mode)


def tail_apply(field, matrix):
    width = field.shape[-1]
    return jnp.dot(field.reshape(-1, width), matrix, precision=precise_mode).reshape(field.shape)


def pair_products(left, right):
    return jnp.dot(left, right.T, precision=precise_mode)


def matmul(left, right):
    return jnp.dot(left, right, precision=precise_mode)


def shards(
    vectors,
    previous,
    beta,
    potential,
    coriolis_fn,
    second_fn,
    rot_const,
    coupling,
    kin_one,
    kin_two,
    kin_three,
    kin_four,
    kin_five,
    kin_six,
    coriolis_derivative,
):
    current = vectors[0]
    older = previous[0]
    block_index = lax.axis_index("ka")
    nblocks = lax.axis_size("ka")
    nvec = current.shape[0]
    first_mat = symmetric(kin_one)
    second_mat = symmetric(kin_two)
    third_mat = symmetric(kin_three)
    eye_four = jnp.eye(kin_four.shape[0], dtype=jnp.float32)
    eye_five = jnp.eye(kin_five.shape[0], dtype=jnp.float32)
    eye_six = jnp.eye(kin_six.shape[0], dtype=jnp.float32)
    eye_outer = jnp.eye(kin_four.shape[0] * kin_five.shape[0], dtype=jnp.float32)
    tail_kinetic = jnp.kron(jnp.kron(symmetric(kin_four), eye_five), eye_six)
    tail_kinetic = tail_kinetic + jnp.kron(jnp.kron(eye_four, symmetric(kin_five)), eye_six)
    tail_kinetic = tail_kinetic + jnp.kron(eye_outer, symmetric(kin_six))
    twist = 0.5 * (coriolis_derivative - coriolis_derivative.T)
    tail_twist = jnp.kron(eye_outer, twist)
    below_one = passed_along(current, "ka", 1)
    above_one = passed_along(current, "ka", -1)
    below_two = passed_along(current, "ka", 2)
    above_two = passed_along(current, "ka", -2)
    flat_grid = current.reshape(nvec, current.shape[1], current.shape[2], -1)
    summed = along_first(
        first_mat, lax.all_to_all(flat_grid, "mode", split_axis=3, concat_axis=1, tiled=True)
    )
    crossed = lax.all_to_all(summed, "mode", split_axis=1, concat_axis=3, tiled=True)
    summed = along_second(
        second_mat, lax.all_to_all(flat_grid, "row", split_axis=3, concat_axis=2, tiled=True)
    )
    crossed = crossed + lax.all_to_all(summed, "row", split_axis=2, concat_axis=3, tiled=True)
    crossed = crossed.reshape(current.shape)
    result = crossed + tail_apply(current, tail_kinetic.T) + along_third(third_mat, current)
    level = (block_index - nblocks // 2).astype(jnp.float32)
    result = result + (potential + rot_const[block_index] * level * level) * current
    near_coef = coupling[0]
    far_coef = coupling[1]
    lower_one = jnp.maximum(block_index - 1, 0)
    lower_two = jnp.maximum(block_index - 2, 0)
    result = result + near_coef[block_index] * coriolis_fn * tail_apply(above_one, tail_twist.T)
    result = result + near_coef[lower_one] * tail_apply(coriolis_fn * below_one, tail_twist)
    result = result + second_fn * (
        far_coef[block_index] * above_two + far_coef[lower_two] * below_two
    )
    result = result - jnp.einsum("ij,jabcr->iabcr", beta, older, precision=precise_mode)
    flat_vec = current.reshape(nvec, -1)
    flat_work = result.reshape(nvec, -1)
    count = float(nblocks * lax.axis_size("mode") * lax.axis_size("row") * flat_vec.shape[1])
    first = lax.psum(pair_products(flat_vec, flat_work), ("ka", "mode", "row")) / count
    flat_work = flat_work - matmul(first.T, flat_vec)
    second = lax.psum(pair_products(flat_vec, flat_work), ("ka", "mode", "row")) / count
    flat_work = flat_work - matmul(second.T, flat_vec)
    gram = lax.psum(pair_products(flat_work, flat_work), ("ka", "mode", "row")) / count
    lower = jnp.linalg.cholesky(gram)
    inverse = jax.scipy.linalg.solve_triangular(lower, jnp.eye(nvec, dtype=jnp.float32), lower=True)
    basis = matmul(inverse, flat_work)
    return (basis.reshape(vectors.shape), first + second, lower)


def solution(mesh):
    return jax.shard_map(
        shards,
        mesh=mesh,
        in_specs=(
            P("ka", None, "mode", "row", None, None),
            P("ka", None, "mode", "row", None, None),
            P(),
            P("mode", "row", None, None),
            P("mode", "row", None, None),
            P("mode", "row", None, None),
            P(),
            P(),
            P(),
            P(),
            P(),
            P(),
            P(),
            P(),
            P(),
        ),
        out_specs=(P("ka", None, "mode", "row", None, None), P(), P()),
        check_vma=False,
    )
```

profile of v0, /device:TPU:1, one launch (start us, length us, event | category | flops | bytes accessed | tf_op | source)
XLA Modules:
  0.0 587.3 jit_solution(8639411634501432942)
XLA Ops:
  0.6 10.1 %copy.99 = f32[1,8,2,4,8,512]{1,3,2,5,4,0:T(4,128)} copy(f32[1,8,2,4,8,512]{5,4,3,2,1,0:T(8,128)} %param.15) | data formatting | bytes 2097152 | tf_op args[0]
  10.8 22.8 %reshape.169 = f32[4,1,65536]{2,1,0:T(1,128)} reshape(f32[4096,2,4,8]{3,2,1,0:T(4,128)} %bitcast.160) | data formatting | bytes 2097152
  33.6 10.3 %all-to-all-start.2 = ((f32[4,1,65536]{2,1,0:T(1,128)}), f32[4,1,65536]{2,1,0:T(1,128)S(1)}, u32[]{:S(2)}, u32[]{:S(2)}) async-start(f32[4,1,65536]{2,1,0:T(1,128)} %reshape.169), calls=%async_computation.2 | async-start | bytes 2097152 | tf_op jit(solution)/shard_map/all_to_all | solution.py:88
  43.9 22.0 %reshape.171 = f32[8,1,32768]{2,1,0:T(1,128)} reshape(f32[4096,2,4,8]{3,2,1,0:T(4,128)} %bitcast.161) | data formatting | bytes 2097152
  65.9 4.7 all-to-all-start
  70.6 4.2 collective-permute-start.1
  76.1 5.0 collective-permute-start.3
  83.5 4.6 reduce.6
  88.2 26.0 %reshape.170 = f32[4096,2,4,8]{3,2,1,0:T(4,128)} reshape(f32[4,65536]{1,0:T(4,128)S(1)} %reduce.6) | data formatting | bytes 2097152
  114.1 13.1 %copy.106 = f32[8,2,4,4,1024]{4,2,3,1,0:T(4,128)S(1)} copy(f32[8,2,4,4,1024]{0,2,1,4,3:T(4,128)} %bitcast.162) | data formatting | bytes 2097152 | tf_op jit(solution)/shard_map/all_to_all | solution.py:88
  132.6 5.4 all-to-all-start.3
  138.2 4.4 reduce.7
  142.6 25.5 %reshape.172 = f32[4096,2,4,8]{3,2,1,0:T(4,128)} reshape(f32[8,32768]{1,0:T(8,128)S(1)} %reduce.7) | data formatting | bytes 2097152
  168.2 9.8 %copy.127 = f32[8,2,4,8,512]{4,3,0,2,1:T(8,128)S(1)} copy(f32[8,2,4,8,512]{0,2,1,4,3:T(4,128)} %bitcast.163) | data formatting | bytes 2097152 | tf_op jit(solution)/shard_map/all_to_all | solution.py:84
  184.4 6.9 %all-to-all-start.1 = ((f32[8,16,4,512]{3,2,0,1:T(4,128)}), f32[8,16,4,512]{3,2,0,1:T(4,128)}, u32[]{:S(2)}, u32[]{:S(2)}) async-start(f32[8,16,4,512]{3,2,0,1:T(4,128)} %copy.102), calls=%async_computation.1 | async-start | bytes 2097152 | tf_op jit(solution)/shard_map/all_to_all | solution.py:86
  191.4 12.1 %multiply_add_fusion = (f32[64,8,64,8]{3,2,1,0:T(8,128)}, f32[64,8,64,8]{3,2,1,0:T(8,128)}) fusion(f32[64,64]{1,0:T(8,128)S(1)} %reshape.162, f32[8,8]{1,0:T(8,128)S(1)} %get-tuple-element.31, f32[64,64]{1,0:T(8,128)S(1)} %fusion.17, f32[8,8]{1,0:T(8,128)S(1)} %fusion.37, f32[8,8]{1,0:T(8,128)S(1)} %get-tuple-element.30), kind=kLoop, calls=%fused_computation.2 | loop fusion | flops 1048576 | bytes 2130688 | tf_op jit(solution)/shard_map/add | solution.py:75
  208.6 13.4 %reshape.166 = f32[512,512,1,1,1]{1,0,2,3,4:T(8,128)} reshape(f32[64,8,64,8]{3,2,1,0:T(8,128)} %get-tuple-element.21) | data formatting | bytes 2097152 | tf_op jit(solution)/shard_map/jit(kron)/mul | solution.py:77
  222.1 13.4 %mul.257 = f32[512,512]{1,0:T(8,128)} reshape(f32[64,8,64,8]{3,2,1,0:T(8,128)} %get-tuple-element.21) | data formatting | bytes 2097152 | tf_op jit(solution)/shard_map/jit(kron)/mul | solution.py:77
  235.6 13.6 %add.110 = f32[512,512]{1,0:T(8,128)} reshape(f32[64,8,64,8]{3,2,1,0:T(8,128)} %get-tuple-element.20) | data formatting | bytes 2097152 | tf_op jit(solution)/shard_map/add | solution.py:75
  253.3 4.4 fusion.51
  266.8 7.3 %fusion.9 = f32[8,2,4,8,512]{4,3,2,1,0:T(8,128)S(1)} fusion(f32[512,512,1,1,1]{1,0,2,3,4:T(8,128)} %reshape.166, f32[8,2,4,8,512]{4,0,3,2,1:T(8,128)} %fusion.13, f32[8,2,4,8,512]{4,3,2,1,0:T(8,128)} %collective-permute-done.3, f32[8,2,4,8,512]{4,3,2,1,0:T(8,128)} %collective-permute-done.2, f32[8,2,4,8,512]{4,3,2,1,0:T(8,128)} %collective-permute-done.1, ...), kind=kOutput, calls=%fused_computation.15 | convolution fusion | flops 1613496320 | bytes 8781836 | tf_op jit(solution)/shard_map/dot_general | solution.py:33
  277.2 105.3 %psum.21 = f32[8,8]{0,1:T(8,128)S(1)} all-reduce(f32[8,8]{0,1:T(8,128)S(1)} %convolution_bitcast_fusion.4), channel_id=1, replica_groups=mesh['ka'=16,'mode'=8,'row'=4] {'ka','mode','row'}, use_global_device_ids=true, to_apply=%region_0.1 | all-reduce | flops 64 | bytes 512 | tf_op jit(solution)/shard_map/psum | solution.py:108
  386.9 93.4 %psum.22 = f32[8,8]{0,1:T(8,128)S(1)} all-reduce(f32[8,8]{0,1:T(8,128)S(1)} %convolution_bitcast_fusion.3), channel_id=1, replica_groups=mesh['ka'=16,'mode'=8,'row'=4] {'ka','mode','row'}, use_global_device_ids=true, to_apply=%region_1.2 | all-reduce | flops 64 | bytes 512 | tf_op jit(solution)/shard_map/psum | solution.py:110
  485.5 95.3 %psum.23 = f32[8,8]{0,1:T(8,128)S(1)} all-reduce(f32[8,8]{0,1:T(8,128)S(1)} %fusion.52), channel_id=1, replica_groups=mesh['ka'=16,'mode'=8,'row'=4] {'ka','mode','row'}, use_global_device_ids=true, to_apply=%region_2.3 | all-reduce | flops 64 | bytes 512 | tf_op jit(solution)/shard_map/psum | solution.py:112
  (93 shorter events, 52.3 us)
Async XLA Ops:
  0.6 204.7 %copy-start = (f32[1,8,2,4,8,512]{5,4,3,2,1,0:T(8,128)S(1)}, f32[1,8,2,4,8,512]{5,4,3,2,1,0:T(8,128)}, u32[]{:S(2)}) copy-start(f32[1,8,2,4,8,512]{5,4,3,2,1,0:T(8,128)} %param.16) | copy-start | bytes 3145732
  10.7 59.8 %copy-start.1 = (f32[1,8,2,4,8,512]{5,4,3,2,1,0:T(8,128)S(1)}, f32[1,8,2,4,8,512]{5,4,3,2,1,0:T(8,128)}, u32[]{:S(2)}) copy-start(f32[1,8,2,4,8,512]{5,4,3,2,1,0:T(8,128)} %param.15) | copy-start | bytes 3145732
  10.7 71.8 %copy-start.9 = (f32[8,8]{1,0:T(8,128)S(1)}, f32[8,8]{1,0:T(8,128)}, u32[]{:S(2)}) copy-start(f32[8,8]{1,0:T(8,128)} %param.26) | copy-start | bytes 772
  10.7 71.9 %copy-start.8 = (f32[8,8]{1,0:T(8,128)S(1)}, f32[8,8]{1,0:T(8,128)}, u32[]{:S(2)}) copy-start(f32[8,8]{1,0:T(8,128)} %param.27) | copy-start | bytes 772
  10.7 72.0 %copy-start.11 = (f32[8,8]{1,0:T(8,128)S(1)}, f32[8,8]{1,0:T(8,128)}, u32[]{:S(2)}) copy-start(f32[8,8]{1,0:T(8,128)} %param.28) | copy-start | bytes 772
  10.7 72.0 %copy-start.10 = (f32[8,8]{1,0:T(8,128)S(1)}, f32[8,8]{1,0:T(8,128)}, u32[]{:S(2)}) copy-start(f32[8,8]{1,0:T(8,128)} %param.29) | copy-start | bytes 772
  10.8 72.1 %copy-start.7 = (f32[16,16]{1,0:T(8,128)S(1)}, f32[16,16]{1,0:T(8,128)}, u32[]{:S(2)}) copy-start(f32[16,16]{1,0:T(8,128)} %param.23) | copy-start | bytes 3076
  10.8 72.2 %copy-start.6 = (f32[16,16]{1,0:T(8,128)S(1)}, f32[16,16]{1,0:T(8,128)}, u32[]{:S(2)}) copy-start(f32[16,16]{1,0:T(8,128)} %param.24) | copy-start | bytes 3076
  33.6 32.3 %all-to-all-start.2 = ((f32[4,1,65536]{2,1,0:T(1,128)}), f32[4,1,65536]{2,1,0:T(1,128)S(1)}, u32[]{:S(2)}, u32[]{:S(2)}) async-start(f32[4,1,65536]{2,1,0:T(1,128)} %reshape.169), calls=%async_computation.2 | async-start | bytes 2097152 | tf_op jit(solution)/shard_map/all_to_all | solution.py:88
  65.9 17.1 %copy-start.3 = (f32[4,1,65536]{2,1,0:T(1,128)}, f32[4,1,65536]{2,1,0:T(1,128)S(1)}, u32[]{:S(2)}) copy-start(f32[4,1,65536]{2,1,0:T(1,128)S(1)} %all-to-all-done.2) | copy-start | bytes 3145732
  65.9 66.7 %all-to-all-start = ((f32[8,1,32768]{2,1,0:T(1,128)}), f32[8,1,32768]{2,1,0:T(1,128)}, u32[]{:S(2)}, u32[]{:S(2)}) async-start(f32[8,1,32768]{2,1,0:T(1,128)} %reshape.171), calls=%async_computation | async-start | bytes 2097152 | tf_op jit(solution)/shard_map/all_to_all | solution.py:84
  70.6 196.2 %collective-permute-start.1 = (f32[8,2,4,8,512]{4,3,2,1,0:T(8,128)S(1)}, f32[8,2,4,8,512]{4,3,2,1,0:T(8,128)}, u32[]{:S(2)}, u32[]{:S(2)}) collective-permute-start(f32[8,2,4,8,512]{4,3,2,1,0:T(8,128)S(1)} %bitcast.164), channel_id=1, source_target_pairs={{0,32},{32,64},{64,96},{96,128},{128,160},{160,192},{192,224},{224... | collective-permute-start | bytes 3145736 | tf_op jit(solution)/shard_map/ppermute | solution.py:12
  74.8 178.5 %collective-permute-start = (f32[8,2,4,8,512]{4,3,2,1,0:T(8,128)S(1)}, f32[8,2,4,8,512]{4,3,2,1,0:T(8,128)}, u32[]{:S(2)}, u32[]{:S(2)}) collective-permute-start(f32[8,2,4,8,512]{4,3,2,1,0:T(8,128)S(1)} %bitcast.165), channel_id=1, source_target_pairs={{32,0},{64,32},{96,64},{128,96},{160,128},{192,160},{224,192},{256... | collective-permute-start | bytes 3145736 | tf_op jit(solution)/shard_map/ppermute | solution.py:12
  76.1 190.7 %collective-permute-start.3 = (f32[8,2,4,8,512]{4,3,2,1,0:T(8,128)S(1)}, f32[8,2,4,8,512]{4,3,2,1,0:T(8,128)}, u32[]{:S(2)}, u32[]{:S(2)}) collective-permute-start(f32[8,2,4,8,512]{4,3,2,1,0:T(8,128)S(1)} %bitcast.166), channel_id=1, source_target_pairs={{0,64},{32,96},{64,128},{96,160},{128,192},{160,224},{192,256},{22... | collective-permute-start | bytes 3145736 | tf_op jit(solution)/shard_map/ppermute | solution.py:12
  81.1 185.7 %collective-permute-start.2 = (f32[8,2,4,8,512]{4,3,2,1,0:T(8,128)S(1)}, f32[8,2,4,8,512]{4,3,2,1,0:T(8,128)}, u32[]{:S(2)}, u32[]{:S(2)}) collective-permute-start(f32[8,2,4,8,512]{4,3,2,1,0:T(8,128)S(1)} %bitcast.167), channel_id=1, source_target_pairs={{64,0},{96,32},{128,64},{160,96},{192,128},{224,160},{256,192},{28... | collective-permute-start | bytes 3145736 | tf_op jit(solution)/shard_map/ppermute | solution.py:12
  132.6 51.8 %all-to-all-start.3 = ((f32[8,2,16,1024]{3,1,0,2:T(2,128)}), f32[8,2,16,1024]{3,1,0,2:T(2,128)}, u32[]{:S(2)}, u32[]{:S(2)}) async-start(f32[8,2,16,1024]{3,1,0,2:T(2,128)} %copy.107), calls=%async_computation.3 | async-start | bytes 2097152 | tf_op jit(solution)/shard_map/all_to_all | solution.py:90
  184.4 78.9 %all-to-all-start.1 = ((f32[8,16,4,512]{3,2,0,1:T(4,128)}), f32[8,16,4,512]{3,2,0,1:T(4,128)}, u32[]{:S(2)}, u32[]{:S(2)}) async-start(f32[8,16,4,512]{3,2,0,1:T(4,128)} %copy.102), calls=%async_computation.1 | async-start | bytes 2097152 | tf_op jit(solution)/shard_map/all_to_all | solution.py:86
  191.3 12.1 %copy-start.14 = (f32[2,16]{1,0:T(2,128)S(1)}, f32[2,16]{1,0:T(2,128)}, u32[]{:S(2)}) copy-start(f32[2,16]{1,0:T(2,128)} %param.22) | copy-start | bytes 388
  191.3 12.1 %copy-start.15 = (f32[16]{0:T(128)S(1)}, f32[16]{0:T(128)}, u32[]{:S(2)}) copy-start(f32[16]{0:T(128)} %param.21) | copy-start | bytes 196
  191.3 14.0 %copy-start.5 = (f32[2,4,8,512]{3,2,1,0:T(8,128)S(1)}, f32[2,4,8,512]{3,2,1,0:T(8,128)}, u32[]{:S(2)}) copy-start(f32[2,4,8,512]{3,2,1,0:T(8,128)} %param.18) | copy-start | bytes 393220
  191.3 14.0 %copy-start.13 = (f32[8,8]{1,0:T(8,128)S(1)}, f32[8,8]{1,0:T(8,128)}, u32[]{:S(2)}) copy-start(f32[8,8]{1,0:T(8,128)} %param.17) | copy-start | bytes 772
  191.3 16.4 %copy-start.4 = (f32[2,4,8,512]{3,2,1,0:T(8,128)S(1)}, f32[2,4,8,512]{3,2,1,0:T(8,128)}, u32[]{:S(2)}) copy-start(f32[2,4,8,512]{3,2,1,0:T(8,128)} %param.19) | copy-start | bytes 393220
  208.6 26.9 %copy-start.12 = (f32[8,8]{1,0:T(8,128)S(1)}, f32[8,8]{1,0:T(8,128)}, u32[]{:S(2)}) copy-start(f32[8,8]{1,0:T(8,128)} %param.25) | copy-start | bytes 772
  383.4 1.0 copy-start.2
where the time goes:
time: 595 us; the launch traced here: 587 us
  blocking collectives  294 us (49%)
  local copies, waits for them, and re-layouts  190 us (32%)
  starting transfers between devices  39.3 us (7%)
  matrix products  36.5 us (6%)
  other arithmetic  25.1 us (4%)
    psum x2, blocking collectives, shards(): lax.psum(pair_products(flat_vec, flat_work), ('ka', 'mode', 'row')) / count  199 us
    unnamed x47, local copies, waits for them, and re-layouts  111 us
    psum x1, blocking collectives, shards(): lax.psum(pair_products(flat_work, flat_work), ('ka', 'mode', 'row')) / count  95.3 us
    mul x2, local copies, waits for them, and re-layouts, shards(): tail_twist = jnp.kron(eye_outer, twist)  26.9 us
    dot_general x3, matrix products, tail_apply(): jnp.dot(field.reshape(-1, width), matrix, precision=precise_mode)  15.8 us
    all_to_all x3, local copies, waits for them, and re-layouts, shards(): lax.all_to_all(flat_grid, 'row', split_axis=3, concat_axis=2, tiled=True)  15 us
    add x1, local copies, waits for them, and re-layouts, shards(): tail_kinetic = tail_kinetic + jnp.kron(eye_outer, symmetric(kin_six))  13.6 us
    all_to_all x3, local copies, waits for them, and re-layouts, shards(): lax.all_to_all(flat_grid, 'mode', split_axis=3, concat_axis=1, tiled=True)  13.5 us
  transfers between devices with their start and end apart: 8, of which 0 were waited for; matrix products, arithmetic and copies ran while one was open for 32% of the time, Pallas kernels for 0%

commit v1 on v0

v1 whole, which is shorter than its diff:
```python
import jax
import jax.numpy as jnp
from jax import lax
from jax.experimental import pallas as pl
from jax.experimental.pallas import tpu as pltpu
from jax.sharding import PartitionSpec as P

F32 = jnp.float32
BF16 = jnp.bfloat16
HI = lax.Precision.HIGHEST
LANES = 128
NT = (((1,), (1,)), ((), ()))


def exact(a, b):
    return jnp.dot(a, b, precision=HI, preferred_element_type=F32)


def exact_nt(a, b):
    return lax.dot_general(a, b, NT, precision=HI, preferred_element_type=F32)


def iota(shape, axis):
    return lax.broadcasted_iota(jnp.int32, shape, axis)


def hot(shape, of):
    return (of(iota(shape, 0)) == iota(shape, 1)).astype(F32)


def halves(x):
    high = x.astype(BF16)
    return high, (x - high.astype(F32)).astype(BF16)


def three_pass(x, high, low):
    xh, xl = halves(x)

    def dot(a, b):
        return jnp.dot(a, b, preferred_element_type=F32)

    return dot(xh, high) + (dot(xl, high) + dot(xh, low))


def splat(table, row):
    return table[pl.ds(row, 8, stride=0), :]


def lane_block(q):
    return pl.ds(q * LANES, LANES)


def spread(rows, left, right, table):
    n = left.shape[1]
    picked = left * (iota((rows, n), 0) % n == iota((rows, n), 1)).astype(F32)
    table[...] = exact(picked, jnp.ones((n, LANES), F32))


def kernel(
    vec,
    prev,
    pot,
    cor,
    sec,
    beta,
    rot,
    coupling,
    kin_one,
    kin_two,
    kin_three,
    kin_four,
    kin_five,
    kin_six,
    deriv,
    out,
    alpha,
    lower,
    v,
    pv,
    po,
    cf,
    sf,
    w,
    zin,
    zout,
    zret,
    rin,
    rout,
    rret,
    yb,
    ob,
    tab1,
    tab2,
    tabb,
    tab3,
    rows4,
    tkh,
    tkl,
    twh,
    twl,
    acc,
    coef,
    arb,
    loc,
    zfs,
    zfr,
    zrs,
    zrr,
    rfs,
    rfr,
    rrs,
    rrr,
    yfs,
    yfr,
    yrs,
    yrr,
    ars,
    arr,
    obs,
):
    ka = lax.axis_index("ka")
    z = lax.axis_index("mode")
    r = lax.axis_index("row")
    x_hi = ka // 8
    y = ka % 8
    nv, n1, n2 = v.shape[0], v.shape[1], v.shape[2]
    u = x_hi * 4 + r
    nblocks = 16

    def local_copy(i, src, dst):
        return pltpu.make_async_copy(src, dst, loc.at[i])

    locals_ = [
        local_copy(0, vec.at[0], v),
        local_copy(1, prev.at[0], pv),
        local_copy(2, pot, po),
        local_copy(3, cor, cf),
        local_copy(4, sec, sf),
        local_copy(5, vec.at[0, z], zin.at[z]),
        local_copy(6, vec.at[0, pl.ds(2 * r, 2)], rin.at[r]),
    ]

    def z_peer(o):
        return {"mode": (z + o) % 8}

    def y_peer(o):
        return {"ka": x_hi * 8 + (y + o) % 8}

    def x_peer(o):
        t = (u + o) % 8
        return {"ka": (t // 4) * 8 + y, "row": t % 4}

    def z_forward(c, o):
        t = (z + o) % 8
        return pltpu.make_async_remote_copy(
            vec.at[0, t, :, c],
            zin.at[z, :, c],
            zfs.at[c, o],
            zfr.at[c, o],
            device_id=z_peer(o),
        )

    def z_back(c, o):
        t = (z + o) % 8
        return pltpu.make_async_remote_copy(
            zout.at[t, :, c],
            zret.at[z, :, c],
            zrs.at[c, o],
            zrr.at[c, o],
            device_id=z_peer(o),
        )

    def r_forward(o):
        t = (r + o) % 4
        return pltpu.make_async_remote_copy(
            vec.at[0, pl.ds(2 * t, 2)],
            rin.at[r],
            rfs.at[o],
            rfr.at[o],
            device_id={"row": t},
        )

    def r_back(o):
        t = (r + o) % 4
        return pltpu.make_async_remote_copy(
            rout.at[t],
            rret.at[pl.ds(2 * r, 2)],
            rrs.at[o],
            rrr.at[o],
            device_id={"row": t},
        )

    def y_own(c, d):
        return pltpu.make_async_remote_copy(
            vec.at[0, :, :, c],
            yb.at[d, :, :, c],
            yfs.at[d, c],
            yfr.at[d, c],
            device_id={"ka": ka + 1 - 2 * d},
        )

    def y_relay(c, d):
        return pltpu.make_async_remote_copy(
            yb.at[d, :, :, c],
            yb.at[d + 2, :, :, c],
            yrs.at[d, c],
            yrr.at[d, c],
            device_id={"ka": ka + 1 - 2 * d},
        )

    can_send = (ka < nblocks - 1, ka > 0)
    has_one = (ka > 0, ka < nblocks - 1)
    has_two = (ka > 1, ka < nblocks - 2)

    barrier = pltpu.get_barrier_semaphore()
    edge = jnp.logical_or(ka == 7, ka == 8)

    @pl.loop(1, 8)
    def _(o):
        pl.semaphore_signal(barrier, inc=1, device_id=z_peer(o))
        pl.semaphore_signal(barrier, inc=1, device_id=y_peer(o))
        pl.semaphore_signal(barrier, inc=1, device_id=x_peer(o))

    @pl.when(edge)
    def _():
        pl.semaphore_signal(barrier, inc=1, device_id={"ka": 15 - ka})

    for copy in locals_:
        copy.start()
    pl.semaphore_wait(barrier, 21 + edge.astype(jnp.int32))

    def start_chunk(c):
        @pl.loop(1, 8)
        def _(o):
            z_forward(c, o).start()

        for d in range(2):

            @pl.when(can_send[d])
            def _():
                y_own(c, d).start()

    start_chunk(0)
    for o in range(1, 4):
        r_forward(o).start()
    for c in range(1, n2):
        start_chunk(c)

    for d in range(2):

        @pl.when(jnp.logical_not(has_one[d]))
        def _():
            yb[d] = jnp.zeros(yb.shape[1:], F32)

        @pl.when(jnp.logical_not(has_two[d]))
        def _():
            yb[d + 2] = jnp.zeros(yb.shape[1:], F32)

    def table_of(matrix, table):
        n = matrix.shape[0]
        pick = hot((n * n, n), lambda q: q // n)
        both = 0.5 * (exact(pick, matrix[...]) + exact_nt(pick, matrix[...]))
        spread(n * n, both, None, table)

    table_of(kin_one, tab1)
    table_of(kin_two, tab2)
    spread(64, exact(hot((64, 8), lambda q: q // 8), beta[...]), None, tabb)
    eye8 = hot((8, 8), lambda q: q)
    sym3 = 0.5 * (kin_three[...] + exact_nt(eye8, kin_three[...]))
    for s in range(8):
        mask = (iota((8, 8), 0) + (8 - s)) % 8 == iota((8, 8), 1)
        tab3[s] = exact(jnp.where(mask, sym3, 0.0), jnp.ones((8, LANES), F32))

    def expand(pick, matrix, pick_t):
        both = 0.5 * (exact(pick, matrix[...]) + exact_nt(pick, matrix[...]))
        return exact_nt(both, pick_t)

    rows4[...] = expand(eye8, kin_four, hot((512, 8), lambda q: q // 64))
    e5 = expand(hot((64, 8), lambda q: q // 8), kin_five, hot((512, 8), lambda q: (q // 8) % 8))
    e6 = expand(hot((64, 8), lambda q: q % 8), kin_six, hot((512, 8), lambda q: q % 8))
    qi = iota((64, 512), 0)
    pi = iota((64, 512), 1)
    m56 = jnp.where(pi % 8 == qi % 8, e5, 0.0) + jnp.where((pi // 8) % 8 == qi // 8, e6, 0.0)
    diag64 = pi % 64 == qi
    for k in range(8):
        block = jnp.where(diag64, rows4[k : k + 1, :], 0.0) + jnp.where(pi // 64 == k, m56, 0.0)
        high, low = halves(block)
        tkh[k * 64 : (k + 1) * 64, :] = high
        tkl[k * 64 : (k + 1) * 64, :] = low
    pick6 = hot((256, 8), lambda q: q % 8)
    turned = 0.5 * (exact_nt(pick6, deriv[...]) - exact(pick6, deriv[...]))
    full = jnp.where(iota((256, 256), 0) // 8 == iota((256, 256), 1) // 8, exact_nt(turned, pick6), 0.0)
    high, low = halves(full)
    twh[...] = high
    twl[...] = low
    acc[...] = jnp.zeros(acc.shape, F32)

    level = (ka - nblocks // 2).astype(F32)
    shift = rot[ka] * level * level
    near = coupling[0, ka]
    near_low = coupling[0, jnp.maximum(ka - 1, 0)]
    far = coupling[1, ka]
    far_low = coupling[1, jnp.maximum(ka - 2, 0)]

    def mix16(load, store, table):
        xs = [[load(b, q) for q in range(2)] for b in range(16)]
        for a in range(16):
            total = None
            for b in range(16):
                k = splat(table, a * 16 + b)
                terms = [k * xs[b][q] for q in range(2)]
                total = terms if total is None else [t + s for t, s in zip(total, terms)]
            for q in range(2):
                store(a, q, total[q])

    def first_mode(c):
        @pl.loop(0, 2)
        def _(h):
            def at(q):
                return pl.ds(pl.multiple_of(h * 256 + q * LANES, LANES), LANES)

            def load(b, q):
                return zin[b // 2, b % 2, c, :, at(q)]

            def store(a, q, val):
                zout[a // 2, a % 2, c, :, at(q)] = val

            mix16(load, store, tab1)

        zret[z, :, c] = zout[z, :, c]

    def second_mode():
        @pl.loop(0, 8)
        def _(k):
            n, m, h = k // 4, (k // 2) % 2, k % 2

            def at(q):
                return pl.ds(pl.multiple_of(h * 256 + q * LANES, LANES), LANES)

            def load(b, q):
                return rin[b // 4, n, m, b % 4, :, at(q)]

            def store(a, q, val):
                rout[a // 4, n, m, a % 4, :, at(q)] = val

            mix16(load, store, tab2)

        rret[pl.ds(2 * r, 2)] = rout[r]

    def gather_products(c, left, right, spots, triangle):
        for g in range(4):
            pairs = [(j, i) for i in (2 * g, 2 * g + 1) for j in range(8) if j <= i or not triangle]
            sums = {}
            for m in range(n1):
                for q in range(4):
                    ls = [left[j, m, c, :, lane_block(q)] for j in range(8)]
                    rs = [right[i, m, c, :, lane_block(q)] for i in (2 * g, 2 * g + 1)]
                    for j, i in pairs:
                        term = ls[j] * rs[i - 2 * g]
                        sums[j, i] = term if (j, i) not in sums else sums[j, i] + term
            for j, i in pairs:
                for spot in spots(j, i):
                    acc[spot * 8 : spot * 8 + 8, :] += sums[j, i]

    def local_terms(c):
        x = v[:, :, c].reshape(nv * n1 * 8, 512)
        w[:, :, c] = three_pass(x, tkh[...], tkl[...]).reshape(nv, n1, 8, 512)

        @pl.loop(0, 4)
        def _(k):
            m, h = k // 2, k % 2
            for q in range(2):
                at = pl.ds(pl.multiple_of(h * 256 + q * LANES, LANES), LANES)
                old = [pv[j, m, c, :, at] for j in range(8)]
                diag = po[m, c, :, at] + shift
                for i in range(8):
                    xi = v[i, m, c, :, at]
                    total = w[i, m, c, :, at] + (diag + tab3[0]) * xi
                    for s in range(1, 8):
                        total = total + tab3[s] * pltpu.roll(xi, s, axis=0)
                    taken = splat(tabb, i * 8) * old[0]
                    for j in range(1, 8):
                        taken = taken + splat(tabb, i * 8 + j) * old[j]
                    w[i, m, c, :, at] = total - taken

        gather_products(c, v, v, lambda j, i: {(8 + j) * 8 + i, (8 + i) * 8 + j}, True)

    def turn(x):
        flat = x.reshape(nv * n1 * 8, 512)
        parts = [three_pass(flat[:, h * 256 : h * 256 + 256], twh[...], twl[...]) for h in range(2)]
        return jnp.concatenate(parts, axis=1).reshape(x.shape)

    def near_terms(c):
        fn = cf[:, c][None]
        above = turn(yb[1, :, :, c])
        w[:, :, c] += (near * fn) * above
        below = turn(fn * yb[0, :, :, c])
        w[:, :, c] -= near_low * below

    def wait_recv_when(cond, copy):
        @pl.when(cond)
        def _():
            copy.wait_recv()

    for copy in locals_:
        copy.wait()

    @pl.loop(0, n2)
    def _(c):
        @pl.loop(1, 8)
        def _(o):
            z_forward(c, o).wait_recv()

        first_mode(c)

        @pl.loop(1, 8)
        def _(o):
            z_back(c, o).start()

        for d in range(2):
            wait_recv_when(has_one[d], y_own(c, d))

            @pl.when(jnp.logical_and(has_one[d], can_send[d]))
            def _():
                y_relay(c, d).start()

        @pl.when(c == 1)
        def _():
            for o in range(1, 4):
                r_forward(o).wait_recv()
            second_mode()
            for o in range(1, 4):
                r_back(o).start()

        local_terms(c)
        near_terms(c)

    for o in range(1, 4):
        r_back(o).wait_recv()

    @pl.loop(0, n2)
    def _(c):
        @pl.loop(1, 8)
        def _(o):
            z_back(c, o).wait_recv()

        for d in range(2):
            wait_recv_when(has_two[d], y_relay(c, d))

        @pl.loop(0, nv)
        def _(n):
            for m in range(n1):
                skip = sf[m, c] * (far * yb[3, n, m, c] + far_low * yb[2, n, m, c])
                w[n, m, c] = (w[n, m, c] + rret[n, m, c]) + (zret[n, m, c] + skip)

        gather_products(c, v, w, lambda j, i: (j * 8 + i, (24 + i) * 8 + j), False)
        gather_products(c, w, w, lambda j, i: {(16 + j) * 8 + i, (16 + i) * 8 + j}, True)

    part = acc[pl.ds(0, 256, stride=8), :]
    for s in range(1, 8):
        part = part + acc[pl.ds(s, 256, stride=8), :]
    sums = jnp.sum(part, axis=1, keepdims=True)
    lane = iota((8, LANES), 1)
    row = iota((8, LANES), 0)
    msg = jnp.zeros((8, LANES), F32)
    for l in range(32):
        msg = jnp.where(lane == l, sums[l * 8 : l * 8 + 8], msg)

    for s, (me, peer) in enumerate(((u, x_peer), (z, z_peer), (y, y_peer))):

        def ar_copy(o, s=s, me=me, peer=peer):
            return pltpu.make_async_remote_copy(
                arb.at[s, me], arb.at[s, me], ars.at[s, o], arr.at[s, o], device_id=peer(o)
            )

        arb[s, me] = msg

        @pl.loop(1, 8)
        def _(o):
            ar_copy(o).start()

        @pl.loop(1, 8)
        def _(o):
            ar_copy(o).wait_recv()

        msg = arb[s, 0]
        for t in range(1, 8):
            msg = msg + arb[s, t]

    msg = msg * (1.0 / float(16 * 8 * 4 * 32768))

    def col(a, k):
        return jnp.broadcast_to(a[:, k : k + 1], (8, LANES))

    def mm(a, b):
        total = col(a, 0) * b[0:1, :]
        for k in range(1, 8):
            total = total + col(a, k) * b[k : k + 1, :]
        return total

    first_t = msg
    overlap = pltpu.roll(msg, LANES - 8, axis=1)
    square = pltpu.roll(msg, LANES - 16, axis=1)
    first = pltpu.roll(msg, LANES - 24, axis=1)
    both_t = 2.0 * first_t - mm(first_t, overlap)
    both = 2.0 * first - mm(overlap, first)
    gram = square - mm(both_t, first) - mm(first_t, both) + mm(mm(both_t, overlap), both)
    alpha[...] = both[:, 0:8]
    work = jnp.where(lane < 8, gram, 0.0)
    work = jnp.where(lane == row + 8, 1.0, work)
    work = jnp.where((lane >= 16) & (lane < 24), pltpu.roll(both_t, 16, axis=1), work)
    factor = jnp.zeros((8, LANES), F32)
    for k in range(8):
        prow = jnp.broadcast_to(work[k : k + 1, :], (8, LANES))
        pivot = col(prow, k)
        column = col(work, k)
        root = lax.rsqrt(pivot)
        factor = jnp.where((lane == k) & (row >= k), column * root, factor)
        below = work - (column / pivot) * prow
        work = jnp.where(row > k, below, jnp.where(row == k, work * root, work))
    lower[...] = factor[:, 0:8]
    for j in range(8):
        coef[j * 8 : j * 8 + 8, :] = col(work, 8 + j)
        coef[64 + j * 8 : 72 + j * 8, :] = -col(work, 16 + j)

    def out_copy(c):
        return pltpu.make_async_copy(ob.at[:, :, c], out.at[0, :, :, c], obs.at[c])

    @pl.loop(0, n2)
    def _(c):
        @pl.loop(0, 4)
        def _(k):
            m, h = k // 2, k % 2
            at = [pl.ds(pl.multiple_of(h * 256 + q * LANES, LANES), LANES) for q in range(2)]
            vs = [[v[j, m, c, :, at[q]] for q in range(2)] for j in range(8)]
            ws = [[w[j, m, c, :, at[q]] for q in range(2)] for j in range(8)]
            for i in range(8):
                total = None
                for base, xs, count in ((64, vs, 8), (0, ws, i + 1)):
                    for j in range(count):
                        k_ = splat(coef, base + j * 8 + i)
                        terms = [k_ * xs[j][q] for q in range(2)]
                        total = terms if total is None else [t + s for t, s in zip(total, terms)]
                for q in range(2):
                    ob[i, m, c, :, at[q]] = total[q]

        out_copy(c).start()

    @pl.loop(0, n2)
    def _(c):
        out_copy(c).wait()

        @pl.loop(1, 8)
        def _(o):
            z_forward(c, o).wait_send()
            z_back(c, o).wait_send()

        for d in range(2):

            @pl.when(can_send[d])
            def _():
                y_own(c, d).wait_send()

            @pl.when(jnp.logical_and(has_one[d], can_send[d]))
            def _():
                y_relay(c, d).wait_send()

    for o in range(1, 4):
        r_forward(o).wait_send()
        r_back(o).wait_send()
    for s, (me, peer) in enumerate(((u, x_peer), (z, z_peer), (y, y_peer))):

        @pl.loop(1, 8)
        def _(o):
            pltpu.make_async_remote_copy(
                arb.at[s, me], arb.at[s, me], ars.at[s, o], arr.at[s, o], device_id=peer(o)
            ).wait_send()


def shards(*args):
    (vectors, previous, beta, potential, coriolis_fn, second_fn, rot_const, coupling, *mats) = args
    block = vectors.shape[1:]
    fn = potential.shape
    any_spec = pl.BlockSpec(memory_space=pl.ANY)
    vmem = pl.BlockSpec(memory_space=pltpu.VMEM)
    smem = pl.BlockSpec(memory_space=pltpu.SMEM)
    nv, n1, n2, n3, nr = block
    dma = pltpu.SemaphoreType.DMA
    scratch = [
        pltpu.VMEM(block, F32),
        pltpu.VMEM(block, F32),
        pltpu.VMEM(fn, F32),
        pltpu.VMEM(fn, F32),
        pltpu.VMEM(fn, F32),
        pltpu.VMEM(block, F32),
        pltpu.VMEM(block, F32),
        pltpu.VMEM(block, F32),
        pltpu.VMEM(block, F32),
        pltpu.VMEM((4, 2) + block[1:], F32),
        pltpu.VMEM((4, 2) + block[1:], F32),
        pltpu.VMEM(block, F32),
        pltpu.VMEM((4,) + block, F32),
        pltpu.VMEM(block, F32),
        pltpu.VMEM((256, LANES), F32),
        pltpu.VMEM((256, LANES), F32),
        pltpu.VMEM((64, LANES), F32),
        pltpu.VMEM((8, 8, LANES), F32),
        pltpu.VMEM((8, nr), F32),
        pltpu.VMEM((nr, nr), BF16),
        pltpu.VMEM((nr, nr), BF16),
        pltpu.VMEM((256, 256), BF16),
        pltpu.VMEM((256, 256), BF16),
        pltpu.VMEM((256 * 8, LANES), F32),
        pltpu.VMEM((128, LANES), F32),
        pltpu.VMEM((3, 8, 8, LANES), F32),
        dma((7,)),
        dma((n2, 8)),
        dma((n2, 8)),
        dma((n2, 8)),
        dma((n2, 8)),
        dma((4,)),
        dma((4,)),
        dma((4,)),
        dma((4,)),
        dma((2, n2)),
        dma((2, n2)),
        dma((2, n2)),
        dma((2, n2)),
        dma((3, 8)),
        dma((3, 8)),
        dma((n2,)),
    ]
    return pl.pallas_call(
        kernel,
        out_shape=(
            jax.ShapeDtypeStruct(vectors.shape, F32),
            jax.ShapeDtypeStruct((nv, nv), F32),
            jax.ShapeDtypeStruct((nv, nv), F32),
        ),
        in_specs=[any_spec] * 5 + [vmem, smem, smem] + [vmem] * 7,
        out_specs=(any_spec, vmem, vmem),
        scratch_shapes=scratch,
        compiler_params=pltpu.CompilerParams(
            collective_id=0, has_side_effects=True, vmem_limit_bytes=48 * 1024 * 1024
        ),
        name="lanczos",
    )(vectors, previous, potential, coriolis_fn, second_fn, beta, rot_const, coupling, *mats)


def solution(mesh):
    split = P("ka", None, "mode", "row", None, None)
    fn = P("mode", "row", None, None)
    return jax.shard_map(
        shards,
        mesh=mesh,
        in_specs=(split, split, P(), fn, fn, fn) + (P(),) * 9,
        out_specs=(split, P(), P()),
        check_vma=False,
    )
```

time: 595 us -> 116 us (0.19); the launches traced: 587 us -> 115 us
  blocking collectives: 294 us -> 0 us
  local copies, waits for them, and re-layouts: 190 us -> 14.2 us
  Pallas kernels: 0 us -> 100 us
  starting transfers between devices: 39.3 us -> 0 us
  matrix products: 36.5 us -> 0 us
  other arithmetic: 25.1 us -> 0 us
    psum x3 -> x0, blocking collectives: 294 us -> none  [the longest x2 199 us: shards(): lax.psum(pair_products(flat_vec, flat_work), ('ka', 'mode', 'row')) / count]
    pallas_call x0 -> x1, Pallas kernels: none -> 100 us  [shards(): pl.pallas_call(kernel, out_shape=(jax.ShapeDtypeStruct(vectors.shape, F32...]
    unnamed x47 -> x33, local copies, waits for them, and re-layouts: 111 us -> 14.2 us
    dot_general x13 -> x0, matrix products: 36.3 us -> none  [the longest x3 15.8 us: tail_apply(): jnp.dot(field.reshape(-1, width), matrix, precision=precise_mode)]
    all_to_all x8 -> x0, local copies, waits for them, and re-layouts: 34.1 us -> none  [the longest x3 15 us: shards(): lax.all_to_all(flat_grid, 'row', split_axis=3, concat_axis=2, tiled=True)]
    all_to_all x4 -> x0, starting transfers between devices: 27.3 us -> none  [the longest x1 10.3 us: shards(): lax.all_to_all(flat_grid, 'row', split_axis=3, concat_axis=2, tiled=True)]
    mul x3 -> x0, local copies, waits for them, and re-layouts: 27 us -> none  [the longest x2 26.9 us: shards(): tail_twist = jnp.kron(eye_outer, twist)]
    add x1 -> x0, local copies, waits for them, and re-layouts: 13.6 us -> none  [shards(): tail_kinetic = tail_kinetic + jnp.kron(eye_outer, symmetric(kin_six))]
  transfers between devices with their start and end apart: 8 -> 0, of which waited for: 0 -> 0; matrix products, arithmetic and copies ran while one was open for 32% -> 0% of each run, Pallas kernels for 0% -> 0%
where the time goes in v1:
time: 116 us; the launch traced here: 115 us
  Pallas kernels  100 us (86%)
  local copies, waits for them, and re-layouts  14.2 us (12%)
    pallas_call x1, Pallas kernels, shards(): pl.pallas_call(kernel, out_shape=(jax.ShapeDtypeStruct(vectors.shape, F32...  100 us
    unnamed x33, local copies, waits for them, and re-layouts  14.2 us

profile of v1, /device:TPU:1, one launch (start us, length us, event | category | flops | bytes accessed | tf_op | source)
XLA Modules:
  0.0 115.3 jit_solution(4472812302622035246)
XLA Ops:
  0.6 0.0 copy-start
  0.6 1.2 %copy-done = f32[1,8,2,4,8,512]{5,4,3,2,1,0:T(8,128)S(1)} copy-done((f32[1,8,2,4,8,512]{5,4,3,2,1,0:T(8,128)S(1)}, f32[1,8,2,4,8,512]{5,4,3,2,1,0:T(8,128)}, u32[]{:S(2)}) %copy-start) | copy-done | bytes 1048600
  1.9 0.0 copy-start.1
  1.9 1.2 %copy-done.1 = f32[1,8,2,4,8,512]{5,4,3,2,1,0:T(8,128)S(1)} copy-done((f32[1,8,2,4,8,512]{5,4,3,2,1,0:T(8,128)S(1)}, f32[1,8,2,4,8,512]{5,4,3,2,1,0:T(8,128)}, u32[]{:S(2)}) %copy-start.1) | copy-done | bytes 1048600
  3.1 0.0 copy-start.2
  3.1 0.9 copy-done.2
  4.0 0.0 copy-start.3
  4.0 0.9 copy-done.3
  4.9 0.0 copy-start.4
  4.9 0.9 copy-done.4
  5.8 0.7 copy-done.5
  6.5 0.7 copy-done.6
  7.2 0.7 copy-done.7
  7.9 0.7 copy-done.8
  8.6 0.7 copy-done.9
  9.3 0.7 copy-done.10
  9.9 0.7 copy-done.11
  10.6 0.7 copy-done.12
  11.3 0.7 copy-done.13
  12.0 0.7 copy-done.14
  12.7 100.5 %lanczos.1 = (f32[1,8,2,4,8,512]{5,4,3,2,1,0:T(8,128)S(1)}, f32[8,8]{1,0:T(8,128)S(1)}, f32[8,8]{1,0:T(8,128)S(1)}) custom-call(f32[1,8,2,4,8,512]{5,4,3,2,1,0:T(8,128)S(1)} %copy-done, f32[1,8,2,4,8,512]{5,4,3,2,1,0:T(8,128)S(1)} %copy-done.1, f32[2,4,8,512]{3,2,1,0:T(8,128)S(1)} %copy-done.2, f32[2,4,8,512]{3,2,1,0:T(8,128)S(1)} %copy-done.3, ...), custom_call_target="tpu_custom_call" | custom-call | tf_op jit(solution)/shard_map/lanczos/pallas_call | solution.py:633
  113.1 1.0 copy.21
  114.1 0.6 copy.22
  114.7 0.6 copy.23
  (10 shorter events, 0.0 us)
Async XLA Ops:
  0.6 1.2 %copy-start = (f32[1,8,2,4,8,512]{5,4,3,2,1,0:T(8,128)S(1)}, f32[1,8,2,4,8,512]{5,4,3,2,1,0:T(8,128)}, u32[]{:S(2)}) copy-start(f32[1,8,2,4,8,512]{5,4,3,2,1,0:T(8,128)} %vec.1) | copy-start | bytes 3145732
  1.9 1.2 %copy-start.1 = (f32[1,8,2,4,8,512]{5,4,3,2,1,0:T(8,128)S(1)}, f32[1,8,2,4,8,512]{5,4,3,2,1,0:T(8,128)}, u32[]{:S(2)}) copy-start(f32[1,8,2,4,8,512]{5,4,3,2,1,0:T(8,128)} %prev.1) | copy-start | bytes 3145732
  3.1 0.9 copy-start.2
  4.0 0.9 copy-start.3
  4.9 0.9 copy-start.4
  5.8 0.7 copy-start.5
  6.5 0.7 copy-start.6
  7.2 0.7 copy-start.7
  7.9 0.7 copy-start.8
  8.6 0.7 copy-start.9
  9.3 0.7 copy-start.10
  9.9 0.7 copy-start.11
  10.6 0.7 copy-start.12
  11.3 0.7 copy-start.13
  12.0 0.7 copy-start.14

commit v2 on v1

--- a/solution.py
+++ b/solution.py
@@ -62,16 +62,16 @@
     pot,
     cor,
     sec,
-    beta,
-    rot,
-    coupling,
-    kin_one,
-    kin_two,
-    kin_three,
-    kin_four,
-    kin_five,
-    kin_six,
-    deriv,
+    beta_hbm,
+    rot_hbm,
+    coupling_hbm,
+    one_hbm,
+    two_hbm,
+    three_hbm,
+    four_hbm,
+    five_hbm,
+    six_hbm,
+    deriv_hbm,
     out,
     alpha,
     lower,
@@ -88,7 +88,18 @@
     rout,
     rret,
     yb,
+    via,
     ob,
+    beta,
+    rot,
+    coupling,
+    kin_one,
+    kin_two,
+    kin_three,
+    kin_four,
+    kin_five,
+    kin_six,
+    deriv,
     tab1,
     tab2,
     tabb,
@@ -114,6 +125,8 @@
     yfr,
     yrs,
     yrr,
+    vr,
+    vs,
     ars,
     arr,
     obs,
@@ -139,6 +152,19 @@
         local_copy(5, vec.at[0, z], zin.at[z]),
         local_copy(6, vec.at[0, pl.ds(2 * r, 2)], rin.at[r]),
     ]
+    small = [
+        (beta_hbm, beta),
+        (rot_hbm, rot),
+        (coupling_hbm, coupling),
+        (one_hbm, kin_one),
+        (two_hbm, kin_two),
+        (three_hbm, kin_three),
+        (four_hbm, kin_four),
+        (five_hbm, kin_five),
+        (six_hbm, kin_six),
+        (deriv_hbm, deriv),
+    ]
+    small = [local_copy(7 + i, *pair) for i, pair in enumerate(small)]
 
     def z_peer(o):
         return {"mode": (z + o) % 8}
@@ -208,6 +234,47 @@
             device_id={"ka": ka + 1 - 2 * d},
         )
 
+    def to_via(k, c, d):
+        src = vec.at[0, :, :, c] if k == 0 else yb.at[d, :, :, c]
+        return pltpu.make_async_remote_copy(
+            src,
+            via.at[k * 2 + c // 2],
+            (yfs, yrs)[k].at[d, c],
+            vr.at[k * 2 + c // 2],
+            device_id={"ka": 15 - 15 * d},
+        )
+
+    def from_via(k, c, d):
+        return pltpu.make_async_remote_copy(
+            via.at[k * 2 + c // 2],
+            yb.at[d + 2 * k, :, :, c],
+            vs.at[k * 2 + c // 2],
+            (yfr, yrr)[k].at[d, c],
+            device_id={"ka": 8 - d},
+        )
+
+    at_edge = (ka == 7, ka == 8)
+    is_via = (ka == 15, ka == 0)
+
+    def send_on(k, c, d, cond):
+        detour = jnp.logical_and(at_edge[d], c % 2 == 1)
+
+        @pl.when(jnp.logical_and(cond, detour))
+        def _():
+            to_via(k, c, d).start()
+
+        @pl.when(jnp.logical_and(cond, jnp.logical_not(detour)))
+        def _():
+            (y_own, y_relay)[k](c, d).start()
+
+    def pass_on(k, c):
+        for d in range(2):
+
+            @pl.when(is_via[d])
+            def _():
+                to_via(k, c, d).wait_recv()
+                from_via(k, c, d).start()
+
     can_send = (ka < nblocks - 1, ka > 0)
     has_one = (ka > 0, ka < nblocks - 1)
     has_two = (ka > 1, ka < nblocks - 2)
@@ -225,7 +292,7 @@
     def _():
         pl.semaphore_signal(barrier, inc=1, device_id={"ka": 15 - ka})
 
-    for copy in locals_:
+    for copy in small + locals_:
         copy.start()
     pl.semaphore_wait(barrier, 21 + edge.astype(jnp.int32))
 
@@ -236,9 +303,7 @@
 
         for d in range(2):
 
-            @pl.when(can_send[d])
-            def _():
-                y_own(c, d).start()
+            send_on(0, c, d, can_send[d])
 
     start_chunk(0)
     for o in range(1, 4):
@@ -255,6 +320,9 @@
         @pl.when(jnp.logical_not(has_two[d]))
         def _():
             yb[d + 2] = jnp.zeros(yb.shape[1:], F32)
+
+    for copy in small:
+        copy.wait()
 
     def table_of(matrix, table):
         n = matrix.shape[0]
@@ -420,9 +488,11 @@
         for d in range(2):
             wait_recv_when(has_one[d], y_own(c, d))
 
-            @pl.when(jnp.logical_and(has_one[d], can_send[d]))
-            def _():
-                y_relay(c, d).start()
+            send_on(1, c, d, jnp.logical_and(has_one[d], can_send[d]))
+
+        @pl.when(c % 2 == 1)
+        def _():
+            pass_on(0, c)
 
         @pl.when(c == 1)
         def _():
@@ -440,6 +510,10 @@
 
     @pl.loop(0, n2)
     def _(c):
+        @pl.when(c < 2)
+        def _():
+            pass_on(1, 2 * c + 1)
+
         @pl.loop(1, 8)
         def _(o):
             z_back(c, o).wait_recv()
@@ -565,6 +639,14 @@
             def _():
                 y_relay(c, d).wait_send()
 
+    for k in range(2):
+        for c in (1, 3):
+            for d in range(2):
+
+                @pl.when(is_via[d])
+                def _():
+                    from_via(k, c, d).wait_send()
+
     for o in range(1, 4):
         r_forward(o).wait_send()
         r_back(o).wait_send()
@@ -581,9 +663,8 @@
     (vectors, previous, beta, potential, coriolis_fn, second_fn, rot_const, coupling, *mats) = args
     block = vectors.shape[1:]
     fn = potential.shape
-    any_spec = pl.BlockSpec(memory_space=pl.ANY)
+    any_spec = pl.BlockSpec(memory_space=pltpu.HBM)
     vmem = pl.BlockSpec(memory_space=pltpu.VMEM)
-    smem = pl.BlockSpec(memory_space=pltpu.SMEM)
     nv, n1, n2, n3, nr = block
     dma = pltpu.SemaphoreType.DMA
     scratch = [
@@ -600,7 +681,14 @@
         pltpu.VMEM((4, 2) + block[1:], F32),
         pltpu.VMEM(block, F32),
         pltpu.VMEM((4,) + block, F32),
+        pltpu.VMEM((4, nv, n1, n3, nr), F32),
         pltpu.VMEM(block, F32),
+        pltpu.VMEM((8, 8), F32),
+        pltpu.SMEM((16,), F32),
+        pltpu.SMEM((2, 16), F32),
+        pltpu.VMEM((16, 16), F32),
+        pltpu.VMEM((16, 16), F32),
+        *[pltpu.VMEM((8, 8), F32)] * 5,
         pltpu.VMEM((256, LANES), F32),
         pltpu.VMEM((256, LANES), F32),
         pltpu.VMEM((64, LANES), F32),
@@ -613,7 +701,7 @@
         pltpu.VMEM((256 * 8, LANES), F32),
         pltpu.VMEM((128, LANES), F32),
         pltpu.VMEM((3, 8, 8, LANES), F32),
-        dma((7,)),
+        dma((17,)),
         dma((n2, 8)),
         dma((n2, 8)),
         dma((n2, 8)),
@@ -626,6 +714,8 @@
         dma((2, n2)),
         dma((2, n2)),
         dma((2, n2)),
+        dma((4,)),
+        dma((4,)),
         dma((3, 8)),
         dma((3, 8)),
         dma((n2,)),
@@ -637,11 +727,11 @@
             jax.ShapeDtypeStruct((nv, nv), F32),
             jax.ShapeDtypeStruct((nv, nv), F32),
         ),
-        in_specs=[any_spec] * 5 + [vmem, smem, smem] + [vmem] * 7,
+        in_specs=[any_spec] * 15,
         out_specs=(any_spec, vmem, vmem),
         scratch_shapes=scratch,
         compiler_params=pltpu.CompilerParams(
-            collective_id=0, has_side_effects=True, vmem_limit_bytes=48 * 1024 * 1024
+            collective_id=0, has_side_effects=True, vmem_limit_bytes=67043328
         ),
         name="lanczos",
     )(vectors, previous, potential, coriolis_fn, second_fn, beta, rot_const, coupling, *mats)

time: 116 us -> 91.8 us (0.79)
  Pallas kernels: 100 us -> 86.9 us
  local copies, waits for them, and re-layouts: 14.2 us -> 3.56 us
    pallas_call x1, Pallas kernels: 100 us -> 86.9 us  [shards(): pl.pallas_call(kernel, out_shape=(jax.ShapeDtypeStruct(vectors.shape, F32...]
    unnamed x33 -> x7, local copies, waits for them, and re-layouts: 14.2 us -> 3.56 us
where the time goes in v2:
time: 91.8 us; the launch traced here: 91.1 us
  Pallas kernels  86.9 us (95%)
  local copies, waits for them, and re-layouts  3.56 us (4%)
    pallas_call x1, Pallas kernels, shards(): pl.pallas_call(kernel, out_shape=(jax.ShapeDtypeStruct(vectors.shape, F32...  86.9 us
    unnamed x7, local copies, waits for them, and re-layouts  3.56 us

profile of v2, /device:TPU:1, one launch (start us, length us, event | category | flops | bytes accessed | tf_op | source)
XLA Modules:
  0.0 91.1 jit_solution(8159910877673155595)
XLA Ops:
  0.6 86.9 %lanczos.1 = (f32[1,8,2,4,8,512]{5,4,3,2,1,0:T(8,128)}, f32[8,8]{1,0:T(8,128)}, f32[8,8]{1,0:T(8,128)}) custom-call(f32[1,8,2,4,8,512]{5,4,3,2,1,0:T(8,128)} %vec.1, f32[1,8,2,4,8,512]{5,4,3,2,1,0:T(8,128)} %prev.1, f32[2,4,8,512]{3,2,1,0:T(8,128)} %pot.1, f32[2,4,8,512]{3,2,1,0:T(8,128)} %cor.1, f32[2,4,8,512]{3,2,1,0:T(8,128)} %sec.1, f32[8,8]{1,0:T(8,128)} %beta_hbm.1, ...), custom_call_target="tpu_custom_call" | custom-call | tf_op jit(solution)/shard_map/lanczos/pallas_call | solution.py:723
  87.5 0.0 copy-start.1
  87.5 2.3 %copy.21 = f32[1,8,2,4,8,512]{5,4,3,2,1,0:T(8,128)} copy(f32[1,8,2,4,8,512]{5,4,3,2,1,0:T(8,128)} %get-tuple-element.6) | data formatting | bytes 2097152
  89.8 0.0 copy-done.1
  89.8 0.0 copy-start
  89.8 0.6 copy.22
  90.4 0.1 copy-done
  90.5 0.6 copy.23
Async XLA Ops:
  87.5 2.3 %copy-start.1 = (f32[8,8]{1,0:T(8,128)S(1)}, f32[8,8]{1,0:T(8,128)}, u32[]{:S(2)}) copy-start(f32[8,8]{1,0:T(8,128)} %get-tuple-element.7) | copy-start | bytes 772
  89.8 0.7 copy-start

commit v3 on v2

--- a/solution.py
+++ b/solution.py
@@ -42,8 +42,16 @@
     return dot(xh, high) + (dot(xl, high) + dot(xh, low))
 
 
+def col(a, k):
+    return jnp.broadcast_to(a[:, k : k + 1], (8, LANES))
+
+
 def splat(table, row):
     return table[pl.ds(row, 8, stride=0), :]
+
+
+def far_first(i):
+    return 4 + (i // 2) * (1 - 2 * (i % 2))
 
 
 def lane_block(q):
@@ -72,9 +80,8 @@
     five_hbm,
     six_hbm,
     deriv_hbm,
-    out,
-    alpha,
-    lower,
+    wout,
+    pack,
     v,
     pv,
     po,
@@ -89,7 +96,6 @@
     rret,
     yb,
     via,
-    ob,
     beta,
     rot,
     coupling,
@@ -110,7 +116,6 @@
     twh,
     twl,
     acc,
-    coef,
     arb,
     loc,
     zfs,
@@ -299,7 +304,7 @@
     def start_chunk(c):
         @pl.loop(1, 8)
         def _(o):
-            z_forward(c, o).start()
+            z_forward(c, far_first(o)).start()
 
         for d in range(2):
 
@@ -483,7 +488,7 @@
 
         @pl.loop(1, 8)
         def _(o):
-            z_back(c, o).start()
+            z_back(c, far_first(o)).start()
 
         for d in range(2):
             wait_recv_when(has_one[d], y_own(c, d))
@@ -494,7 +499,7 @@
         def _():
             pass_on(0, c)
 
-        @pl.when(c == 1)
+        @pl.when(c == 2)
         def _():
             for o in range(1, 4):
                 r_forward(o).wait_recv()
@@ -505,15 +510,16 @@
         local_terms(c)
         near_terms(c)
 
+    def w_copy(c):
+        return pltpu.make_async_copy(w.at[:, :, c], wout.at[:, :, c], obs.at[c])
+
+    for c in (1, 3):
+        pass_on(1, c)
     for o in range(1, 4):
         r_back(o).wait_recv()
 
     @pl.loop(0, n2)
     def _(c):
-        @pl.when(c < 2)
-        def _():
-            pass_on(1, 2 * c + 1)
-
         @pl.loop(1, 8)
         def _(o):
             z_back(c, o).wait_recv()
@@ -527,6 +533,7 @@
                 skip = sf[m, c] * (far * yb[3, n, m, c] + far_low * yb[2, n, m, c])
                 w[n, m, c] = (w[n, m, c] + rret[n, m, c]) + (zret[n, m, c] + skip)
 
+        w_copy(c).start()
         gather_products(c, v, w, lambda j, i: (j * 8 + i, (24 + i) * 8 + j), False)
         gather_products(c, w, w, lambda j, i: {(16 + j) * 8 + i, (16 + i) * 8 + j}, True)
 
@@ -563,9 +570,6 @@
 
     msg = msg * (1.0 / float(16 * 8 * 4 * 32768))
 
-    def col(a, k):
-        return jnp.broadcast_to(a[:, k : k + 1], (8, LANES))
-
     def mm(a, b):
         total = col(a, 0) * b[0:1, :]
         for k in range(1, 8):
@@ -579,7 +583,6 @@
     both_t = 2.0 * first_t - mm(first_t, overlap)
     both = 2.0 * first - mm(overlap, first)
     gram = square - mm(both_t, first) - mm(first_t, both) + mm(mm(both_t, overlap), both)
-    alpha[...] = both[:, 0:8]
     work = jnp.where(lane < 8, gram, 0.0)
     work = jnp.where(lane == row + 8, 1.0, work)
     work = jnp.where((lane >= 16) & (lane < 24), pltpu.roll(both_t, 16, axis=1), work)
@@ -592,16 +595,85 @@
         factor = jnp.where((lane == k) & (row >= k), column * root, factor)
         below = work - (column / pivot) * prow
         work = jnp.where(row > k, below, jnp.where(row == k, work * root, work))
-    lower[...] = factor[:, 0:8]
+    pack[0] = work
+    pack[1] = both
+    pack[2] = factor
+
+    @pl.loop(0, n2)
+    def _(c):
+        w_copy(c).wait()
+
+        @pl.loop(1, 8)
+        def _(o):
+            z_forward(c, o).wait_send()
+            z_back(c, o).wait_send()
+
+        for d in range(2):
+
+            @pl.when(can_send[d])
+            def _():
+                y_own(c, d).wait_send()
+
+            @pl.when(jnp.logical_and(has_one[d], can_send[d]))
+            def _():
+                y_relay(c, d).wait_send()
+
+    for k in range(2):
+        for c in (1, 3):
+            for d in range(2):
+
+                @pl.when(is_via[d])
+                def _():
+                    from_via(k, c, d).wait_send()
+
+    for o in range(1, 4):
+        r_forward(o).wait_send()
+        r_back(o).wait_send()
+    for s, (me, peer) in enumerate(((u, x_peer), (z, z_peer), (y, y_peer))):
+
+        @pl.loop(1, 8)
+        def _(o):
+            pltpu.make_async_remote_copy(
+                arb.at[s, me], arb.at[s, me], ars.at[s, o], arr.at[s, o], device_id=peer(o)
+            ).wait_send()
+
+
+def finish(vec, wfin, pack_hbm, out, alpha_hbm, lower_hbm, v, w, ob, pack, coef, small, sem):
+    n2 = v.shape[2]
+
+    def loads(c):
+        return (
+            pltpu.make_async_copy(vec.at[0, :, :, c], v.at[:, :, c], sem.at[0, c]),
+            pltpu.make_async_copy(wfin.at[:, :, c], w.at[:, :, c], sem.at[1, c]),
+        )
+
+    first = pltpu.make_async_copy(pack_hbm, pack, sem.at[3, 0])
+    first.start()
+    for c in range(n2):
+        for copy in loads(c):
+            copy.start()
+    first.wait()
+    small[0] = pack[1, :, 0:8]
+    small[1] = pack[2, :, 0:8]
+    tiny = [
+        pltpu.make_async_copy(small.at[0], alpha_hbm, sem.at[3, 1]),
+        pltpu.make_async_copy(small.at[1], lower_hbm, sem.at[3, 2]),
+    ]
+    for copy in tiny:
+        copy.start()
+    work = pack[0]
     for j in range(8):
         coef[j * 8 : j * 8 + 8, :] = col(work, 8 + j)
         coef[64 + j * 8 : 72 + j * 8, :] = -col(work, 16 + j)
 
     def out_copy(c):
-        return pltpu.make_async_copy(ob.at[:, :, c], out.at[0, :, :, c], obs.at[c])
+        return pltpu.make_async_copy(ob.at[:, :, c], out.at[0, :, :, c], sem.at[2, c])
 
     @pl.loop(0, n2)
     def _(c):
+        for copy in loads(c):
+            copy.wait()
+
         @pl.loop(0, 4)
         def _(k):
             m, h = k // 2, k % 2
@@ -612,8 +684,8 @@
                 total = None
                 for base, xs, count in ((64, vs, 8), (0, ws, i + 1)):
                     for j in range(count):
-                        k_ = splat(coef, base + j * 8 + i)
-                        terms = [k_ * xs[j][q] for q in range(2)]
+                        factor = splat(coef, base + j * 8 + i)
+                        terms = [factor * xs[j][q] for q in range(2)]
                         total = terms if total is None else [t + s for t, s in zip(total, terms)]
                 for q in range(2):
                     ob[i, m, c, :, at[q]] = total[q]
@@ -624,39 +696,8 @@
     def _(c):
         out_copy(c).wait()
 
-        @pl.loop(1, 8)
-        def _(o):
-            z_forward(c, o).wait_send()
-            z_back(c, o).wait_send()
-
-        for d in range(2):
-
-            @pl.when(can_send[d])
-            def _():
-                y_own(c, d).wait_send()
-
-            @pl.when(jnp.logical_and(has_one[d], can_send[d]))
-            def _():
-                y_relay(c, d).wait_send()
-
-    for k in range(2):
-        for c in (1, 3):
-            for d in range(2):
-
-                @pl.when(is_via[d])
-                def _():
-                    from_via(k, c, d).wait_send()
-
-    for o in range(1, 4):
-        r_forward(o).wait_send()
-        r_back(o).wait_send()
-    for s, (me, peer) in enumerate(((u, x_peer), (z, z_peer), (y, y_peer))):
-
-        @pl.loop(1, 8)
-        def _(o):
-            pltpu.make_async_remote_copy(
-                arb.at[s, me], arb.at[s, me], ars.at[s, o], arr.at[s, o], device_id=peer(o)
-            ).wait_send()
+    for copy in tiny:
+        copy.wait()
 
 
 def shards(*args):
@@ -682,7 +723,6 @@
         pltpu.VMEM(block, F32),
         pltpu.VMEM((4,) + block, F32),
         pltpu.VMEM((4, nv, n1, n3, nr), F32),
-        pltpu.VMEM(block, F32),
         pltpu.VMEM((8, 8), F32),
         pltpu.SMEM((16,), F32),
         pltpu.SMEM((2, 16), F32),
@@ -699,7 +739,6 @@
         pltpu.VMEM((256, 256), BF16),
         pltpu.VMEM((256, 256), BF16),
         pltpu.VMEM((256 * 8, LANES), F32),
-        pltpu.VMEM((128, LANES), F32),
         pltpu.VMEM((3, 8, 8, LANES), F32),
         dma((17,)),
         dma((n2, 8)),
@@ -720,21 +759,41 @@
         dma((3, 8)),
         dma((n2,)),
     ]
-    return pl.pallas_call(
+    wfin, pack = pl.pallas_call(
         kernel,
         out_shape=(
-            jax.ShapeDtypeStruct(vectors.shape, F32),
-            jax.ShapeDtypeStruct((nv, nv), F32),
-            jax.ShapeDtypeStruct((nv, nv), F32),
+            jax.ShapeDtypeStruct(block, F32),
+            jax.ShapeDtypeStruct((3, nv, LANES), F32),
         ),
         in_specs=[any_spec] * 15,
-        out_specs=(any_spec, vmem, vmem),
+        out_specs=(any_spec, vmem),
         scratch_shapes=scratch,
         compiler_params=pltpu.CompilerParams(
             collective_id=0, has_side_effects=True, vmem_limit_bytes=67043328
         ),
         name="lanczos",
     )(vectors, previous, potential, coriolis_fn, second_fn, beta, rot_const, coupling, *mats)
+    return pl.pallas_call(
+        finish,
+        out_shape=(
+            jax.ShapeDtypeStruct(vectors.shape, F32),
+            jax.ShapeDtypeStruct((nv, nv), F32),
+            jax.ShapeDtypeStruct((nv, nv), F32),
+        ),
+        in_specs=[any_spec] * 3,
+        out_specs=(any_spec,) * 3,
+        scratch_shapes=[
+            pltpu.VMEM(block, F32),
+            pltpu.VMEM(block, F32),
+            pltpu.VMEM(block, F32),
+            pltpu.VMEM((3, nv, LANES), F32),
+            pltpu.VMEM((128, LANES), F32),
+            pltpu.VMEM((2, nv, nv), F32),
+            dma((4, n2)),
+        ],
+        compiler_params=pltpu.CompilerParams(vmem_limit_bytes=67043328),
+        name="basis",
+    )(vectors, wfin, pack)
 
 
 def solution(mesh):

time: 91.8 us -> 88.3 us (0.962)
  local copies, waits for them, and re-layouts: 3.56 us -> 0 us
    unnamed x7 -> x0, local copies, waits for them, and re-layouts: 3.56 us -> none
    pallas_call x1 -> x2, Pallas kernels: 86.9 us -> 87.1 us  [the longest x1 84.2 us: shards(): pl.pallas_call(kernel, out_shape=(jax.ShapeDtypeStruct(block, F32), jax.S...]
where the time goes in v3:
time: 88.3 us; the launch traced here: 87.8 us
  Pallas kernels  87.1 us (99%)
    pallas_call x1, Pallas kernels, shards(): pl.pallas_call(kernel, out_shape=(jax.ShapeDtypeStruct(block, F32), jax.S...  84.2 us
    pallas_call x1, Pallas kernels, shards(): pl.pallas_call(finish, out_shape=(jax.ShapeDtypeStruct(vectors.shape, F32...  2.98 us

profile of v3, /device:TPU:1, one launch (start us, length us, event | category | flops | bytes accessed | tf_op | source)
XLA Modules:
  0.0 87.8 jit_solution(11252479323689755801)
XLA Ops:
  0.6 84.2 %lanczos.1 = (f32[8,2,4,8,512]{4,3,2,1,0:T(8,128)}, f32[3,8,128]{2,1,0:T(8,128)}) custom-call(f32[1,8,2,4,8,512]{5,4,3,2,1,0:T(8,128)} %vec.3, f32[1,8,2,4,8,512]{5,4,3,2,1,0:T(8,128)} %prev.1, f32[2,4,8,512]{3,2,1,0:T(8,128)} %pot.1, f32[2,4,8,512]{3,2,1,0:T(8,128)} %cor.1, f32[2,4,8,512]{3,2,1,0:T(8,128)} %sec.1, f32[8,8]{1,0:T(8,128)} %beta_hbm.1, ...), custom_call_target="tpu_custom_call" | custom-call | tf_op jit(solution)/shard_map/lanczos/pallas_call | solution.py:762
  84.8 3.0 %basis.1 = (f32[1,8,2,4,8,512]{5,4,3,2,1,0:T(8,128)}, f32[8,8]{1,0:T(8,128)}, f32[8,8]{1,0:T(8,128)}) custom-call(f32[1,8,2,4,8,512]{5,4,3,2,1,0:T(8,128)} %vec.3, f32[8,2,4,8,512]{4,3,2,1,0:T(8,128)} %get-tuple-element.5.wfin, f32[3,8,128]{2,1,0:T(8,128)} %get-tuple-element.6.pack_hbm), custom_call_target="tpu_custom_call" | custom-call | tf_op jit(solution)/shard_map/basis/pallas_call | solution.py:776

commit v4 on v3

--- a/solution.py
+++ b/solution.py
@@ -116,6 +116,7 @@
     twh,
     twl,
     acc,
+    total,
     arb,
     loc,
     zfs,
@@ -287,18 +288,14 @@
     barrier = pltpu.get_barrier_semaphore()
     edge = jnp.logical_or(ka == 7, ka == 8)
 
-    @pl.loop(1, 8)
-    def _(o):
-        pl.semaphore_signal(barrier, inc=1, device_id=z_peer(o))
-        pl.semaphore_signal(barrier, inc=1, device_id=y_peer(o))
-        pl.semaphore_signal(barrier, inc=1, device_id=x_peer(o))
+    for i in range(1, 8):
+        for peer in (z_peer, y_peer, x_peer):
+            pl.semaphore_signal(barrier, inc=1, device_id=peer(far_first(i)))
 
     @pl.when(edge)
     def _():
         pl.semaphore_signal(barrier, inc=1, device_id={"ka": 15 - ka})
 
-    for copy in small + locals_:
-        copy.start()
     pl.semaphore_wait(barrier, 21 + edge.astype(jnp.int32))
 
     def start_chunk(c):
@@ -313,6 +310,8 @@
     start_chunk(0)
     for o in range(1, 4):
         r_forward(o).start()
+    for copy in small + locals_:
+        copy.start()
     for c in range(1, n2):
         start_chunk(c)
 
@@ -456,7 +455,7 @@
                         taken = taken + splat(tabb, i * 8 + j) * old[j]
                     w[i, m, c, :, at] = total - taken
 
-        gather_products(c, v, v, lambda j, i: {(8 + j) * 8 + i, (8 + i) * 8 + j}, True)
+        gather_products(c, v, v, lambda j, i: {(24 + j) * 8 + i, (24 + i) * 8 + j}, True)
 
     def turn(x):
         flat = x.reshape(nv * n1 * 8, 512)
@@ -510,11 +509,70 @@
         local_terms(c)
         near_terms(c)
 
+    lane = iota((8, LANES), 1)
+    row = iota((8, LANES), 0)
+
+    def sum_into(count, shift, at):
+        rows = count * 8
+        part = acc[pl.ds(at * 64, rows, stride=8), :]
+        for s in range(1, 8):
+            part = part + acc[pl.ds(at * 64 + s, rows, stride=8), :]
+        sums = jnp.sum(part, axis=1, keepdims=True)
+        msg = total[...]
+        for l in range(count):
+            msg = jnp.where(lane == l + shift, sums[l * 8 : l * 8 + 8], msg)
+        total[...] = msg
+
+    total[...] = jnp.zeros((8, LANES), F32)
+    sum_into(8, 0, 24)
+
     def w_copy(c):
         return pltpu.make_async_copy(w.at[:, :, c], wout.at[:, :, c], obs.at[c])
 
     for c in (1, 3):
         pass_on(1, c)
+
+    @pl.loop(0, n2)
+    def _(c):
+        @pl.loop(1, 8)
+        def _(o):
+            z_forward(c, o).wait_send()
+
+        for d in range(2):
+
+            @pl.when(can_send[d])
+            def _():
+                y_own(c, d).wait_send()
+
+    for o in range(1, 4):
+        r_forward(o).wait_send()
+
+    def wait_sends_back():
+        @pl.loop(0, n2)
+        def _(c):
+            w_copy(c).wait()
+
+            @pl.loop(1, 8)
+            def _(o):
+                z_back(c, o).wait_send()
+
+            for d in range(2):
+
+                @pl.when(jnp.logical_and(has_one[d], can_send[d]))
+                def _():
+                    y_relay(c, d).wait_send()
+
+        for k in range(2):
+            for c in (1, 3):
+                for d in range(2):
+
+                    @pl.when(is_via[d])
+                    def _():
+                        from_via(k, c, d).wait_send()
+
+        for o in range(1, 4):
+            r_back(o).wait_send()
+
     for o in range(1, 4):
         r_back(o).wait_recv()
 
@@ -534,39 +592,34 @@
                 w[n, m, c] = (w[n, m, c] + rret[n, m, c]) + (zret[n, m, c] + skip)
 
         w_copy(c).start()
-        gather_products(c, v, w, lambda j, i: (j * 8 + i, (24 + i) * 8 + j), False)
-        gather_products(c, w, w, lambda j, i: {(16 + j) * 8 + i, (16 + i) * 8 + j}, True)
-
-    part = acc[pl.ds(0, 256, stride=8), :]
-    for s in range(1, 8):
-        part = part + acc[pl.ds(s, 256, stride=8), :]
-    sums = jnp.sum(part, axis=1, keepdims=True)
-    lane = iota((8, LANES), 1)
-    row = iota((8, LANES), 0)
-    msg = jnp.zeros((8, LANES), F32)
-    for l in range(32):
-        msg = jnp.where(lane == l, sums[l * 8 : l * 8 + 8], msg)
-
-    for s, (me, peer) in enumerate(((u, x_peer), (z, z_peer), (y, y_peer))):
-
-        def ar_copy(o, s=s, me=me, peer=peer):
-            return pltpu.make_async_remote_copy(
-                arb.at[s, me], arb.at[s, me], ars.at[s, o], arr.at[s, o], device_id=peer(o)
-            )
-
-        arb[s, me] = msg
-
-        @pl.loop(1, 8)
-        def _(o):
-            ar_copy(o).start()
-
-        @pl.loop(1, 8)
-        def _(o):
-            ar_copy(o).wait_recv()
-
-        msg = arb[s, 0]
+        gather_products(c, v, w, lambda j, i: (j * 8 + i, (16 + i) * 8 + j), False)
+        gather_products(c, w, w, lambda j, i: {(8 + j) * 8 + i, (8 + i) * 8 + j}, True)
+
+    sum_into(24, 8, 0)
+    msg = total[...]
+
+    groups = ((u, x_peer), (z, z_peer), (y, y_peer))
+
+    def ar_copy(g, o):
+        me, peer = groups[g]
+        return pltpu.make_async_remote_copy(
+            arb.at[g, me], arb.at[g, me], ars.at[g, o], arr.at[g, o], device_id=peer(o)
+        )
+
+    for g in range(3):
+        arb[g, groups[g][0]] = msg
+        for i in range(1, 8):
+            ar_copy(g, far_first(i)).start()
+        if g == 0:
+            wait_sends_back()
+        else:
+            for i in range(1, 8):
+                ar_copy(g - 1, i).wait_send()
+        for i in range(1, 8):
+            ar_copy(g, i).wait_recv()
+        msg = arb[g, 0]
         for t in range(1, 8):
-            msg = msg + arb[s, t]
+            msg = msg + arb[g, t]
 
     msg = msg * (1.0 / float(16 * 8 * 4 * 32768))
 
@@ -576,8 +629,8 @@
             total = total + col(a, k) * b[k : k + 1, :]
         return total
 
-    first_t = msg
-    overlap = pltpu.roll(msg, LANES - 8, axis=1)
+    overlap = msg
+    first_t = pltpu.roll(msg, LANES - 8, axis=1)
     square = pltpu.roll(msg, LANES - 16, axis=1)
     first = pltpu.roll(msg, LANES - 24, axis=1)
     both_t = 2.0 * first_t - mm(first_t, overlap)
@@ -599,43 +652,8 @@
     pack[1] = both
     pack[2] = factor
 
-    @pl.loop(0, n2)
-    def _(c):
-        w_copy(c).wait()
-
-        @pl.loop(1, 8)
-        def _(o):
-            z_forward(c, o).wait_send()
-            z_back(c, o).wait_send()
-
-        for d in range(2):
-
-            @pl.when(can_send[d])
-            def _():
-                y_own(c, d).wait_send()
-
-            @pl.when(jnp.logical_and(has_one[d], can_send[d]))
-            def _():
-                y_relay(c, d).wait_send()
-
-    for k in range(2):
-        for c in (1, 3):
-            for d in range(2):
-
-                @pl.when(is_via[d])
-                def _():
-                    from_via(k, c, d).wait_send()
-
-    for o in range(1, 4):
-        r_forward(o).wait_send()
-        r_back(o).wait_send()
-    for s, (me, peer) in enumerate(((u, x_peer), (z, z_peer), (y, y_peer))):
-
-        @pl.loop(1, 8)
-        def _(o):
-            pltpu.make_async_remote_copy(
-                arb.at[s, me], arb.at[s, me], ars.at[s, o], arr.at[s, o], device_id=peer(o)
-            ).wait_send()
+    for i in range(1, 8):
+        ar_copy(2, i).wait_send()
 
 
 def finish(vec, wfin, pack_hbm, out, alpha_hbm, lower_hbm, v, w, ob, pack, coef, small, sem):
@@ -739,6 +757,7 @@
         pltpu.VMEM((256, 256), BF16),
         pltpu.VMEM((256, 256), BF16),
         pltpu.VMEM((256 * 8, LANES), F32),
+        pltpu.VMEM((8, LANES), F32),
         pltpu.VMEM((3, 8, 8, LANES), F32),
         dma((17,)),
         dma((n2, 8)),

time: 88.3 us -> 87.1 us (0.986)
  the two profiles are of different devices: /device:TPU:1 before, /device:TPU:2 now
where the time goes in v4:
time: 87.1 us; the launch traced here: 86.9 us
  Pallas kernels  86.2 us (99%)
    pallas_call x1, Pallas kernels, shards(): pl.pallas_call(kernel, out_shape=(jax.ShapeDtypeStruct(block, F32), jax.S...  83.3 us
    pallas_call x1, Pallas kernels, shards(): pl.pallas_call(finish, out_shape=(jax.ShapeDtypeStruct(vectors.shape, F32...  2.98 us

profile of v4, /device:TPU:2, one launch (start us, length us, event | category | flops | bytes accessed | tf_op | source)
XLA Modules:
  0.0 86.9 jit_solution(15923451234370947560)
XLA Ops:
  0.6 83.3 %lanczos.1 = (f32[8,2,4,8,512]{4,3,2,1,0:T(8,128)}, f32[3,8,128]{2,1,0:T(8,128)}) custom-call(f32[1,8,2,4,8,512]{5,4,3,2,1,0:T(8,128)} %vec.3, f32[1,8,2,4,8,512]{5,4,3,2,1,0:T(8,128)} %prev.1, f32[2,4,8,512]{3,2,1,0:T(8,128)} %pot.1, f32[2,4,8,512]{3,2,1,0:T(8,128)} %cor.1, f32[2,4,8,512]{3,2,1,0:T(8,128)} %sec.1, f32[8,8]{1,0:T(8,128)} %beta_hbm.1, ...), custom_call_target="tpu_custom_call" | custom-call | tf_op jit(solution)/shard_map/lanczos/pallas_call | solution.py:781
  83.9 3.0 %basis.1 = (f32[1,8,2,4,8,512]{5,4,3,2,1,0:T(8,128)}, f32[8,8]{1,0:T(8,128)}, f32[8,8]{1,0:T(8,128)}) custom-call(f32[1,8,2,4,8,512]{5,4,3,2,1,0:T(8,128)} %vec.3, f32[8,2,4,8,512]{4,3,2,1,0:T(8,128)} %get-tuple-element.5.wfin, f32[3,8,128]{2,1,0:T(8,128)} %get-tuple-element.6.pack_hbm), custom_call_target="tpu_custom_call" | custom-call | tf_op jit(solution)/shard_map/basis/pallas_call | solution.py:795

commit v5 on v4

--- a/solution.py
+++ b/solution.py
@@ -9,6 +9,7 @@
 BF16 = jnp.bfloat16
 HI = lax.Precision.HIGHEST
 LANES = 128
+VIA = 2
 NT = (((1,), (1,)), ((), ()))
 
 
@@ -244,17 +245,17 @@
         src = vec.at[0, :, :, c] if k == 0 else yb.at[d, :, :, c]
         return pltpu.make_async_remote_copy(
             src,
-            via.at[k * 2 + c // 2],
+            via.at[k * n2 + c],
             (yfs, yrs)[k].at[d, c],
-            vr.at[k * 2 + c // 2],
+            vr.at[k * n2 + c],
             device_id={"ka": 15 - 15 * d},
         )
 
     def from_via(k, c, d):
         return pltpu.make_async_remote_copy(
-            via.at[k * 2 + c // 2],
+            via.at[k * n2 + c],
             yb.at[d + 2 * k, :, :, c],
-            vs.at[k * 2 + c // 2],
+            vs.at[k * n2 + c],
             (yfr, yrr)[k].at[d, c],
             device_id={"ka": 8 - d},
         )
@@ -263,7 +264,7 @@
     is_via = (ka == 15, ka == 0)
 
     def send_on(k, c, d, cond):
-        detour = jnp.logical_and(at_edge[d], c % 2 == 1)
+        detour = jnp.logical_and(at_edge[d], c < VIA)
 
         @pl.when(jnp.logical_and(cond, detour))
         def _():
@@ -307,9 +308,9 @@
 
             send_on(0, c, d, can_send[d])
 
-    start_chunk(0)
     for o in range(1, 4):
         r_forward(o).start()
+    start_chunk(0)
     for copy in small + locals_:
         copy.start()
     for c in range(1, n2):
@@ -494,11 +495,11 @@
 
             send_on(1, c, d, jnp.logical_and(has_one[d], can_send[d]))
 
-        @pl.when(c % 2 == 1)
+        @pl.when(c < VIA)
         def _():
             pass_on(0, c)
 
-        @pl.when(c == 2)
+        @pl.when(c == 1)
         def _():
             for o in range(1, 4):
                 r_forward(o).wait_recv()
@@ -518,18 +519,22 @@
         for s in range(1, 8):
             part = part + acc[pl.ds(at * 64 + s, rows, stride=8), :]
         sums = jnp.sum(part, axis=1, keepdims=True)
-        msg = total[...]
-        for l in range(count):
-            msg = jnp.where(lane == l + shift, sums[l * 8 : l * 8 + 8], msg)
-        total[...] = msg
-
-    total[...] = jnp.zeros((8, LANES), F32)
+        for a in range(2):
+            packed = total[a]
+            for l in range(count):
+                q = l + shift
+                if q // 16 == a:
+                    here = lane == row + (q % 16) * 8
+                    packed = jnp.where(here, sums[l * 8 : l * 8 + 8], packed)
+            total[a] = packed
+
+    total[...] = jnp.zeros((2, 8, LANES), F32)
     sum_into(8, 0, 24)
 
     def w_copy(c):
         return pltpu.make_async_copy(w.at[:, :, c], wout.at[:, :, c], obs.at[c])
 
-    for c in (1, 3):
+    for c in range(VIA):
         pass_on(1, c)
 
     @pl.loop(0, n2)
@@ -563,7 +568,7 @@
                     y_relay(c, d).wait_send()
 
         for k in range(2):
-            for c in (1, 3):
+            for c in range(VIA):
                 for d in range(2):
 
                     @pl.when(is_via[d])
@@ -596,7 +601,7 @@
         gather_products(c, w, w, lambda j, i: {(8 + j) * 8 + i, (8 + i) * 8 + j}, True)
 
     sum_into(24, 8, 0)
-    msg = total[...]
+    msg = jnp.concatenate([jnp.sum(total[a], axis=0, keepdims=True) for a in range(2)], axis=0)
 
     groups = ((u, x_peer), (z, z_peer), (y, y_peer))
 
@@ -629,10 +634,12 @@
             total = total + col(a, k) * b[k : k + 1, :]
         return total
 
-    overlap = msg
-    first_t = pltpu.roll(msg, LANES - 8, axis=1)
-    square = pltpu.roll(msg, LANES - 16, axis=1)
-    first = pltpu.roll(msg, LANES - 24, axis=1)
+    own = [jnp.where(lane % 8 == row, msg[a : a + 1, :], 0.0) for a in range(2)]
+    whole = exact(jnp.concatenate(own, axis=0), hot((LANES, LANES), lambda q: q // 8))
+    overlap = whole[0:8]
+    first_t = pltpu.roll(overlap, LANES - 8, axis=1)
+    square = whole[8:16]
+    first = pltpu.roll(square, LANES - 8, axis=1)
     both_t = 2.0 * first_t - mm(first_t, overlap)
     both = 2.0 * first - mm(overlap, first)
     gram = square - mm(both_t, first) - mm(first_t, both) + mm(mm(both_t, overlap), both)
@@ -740,7 +747,7 @@
         pltpu.VMEM((4, 2) + block[1:], F32),
         pltpu.VMEM(block, F32),
         pltpu.VMEM((4,) + block, F32),
-        pltpu.VMEM((4, nv, n1, n3, nr), F32),
+        pltpu.VMEM((2 * n2, nv, n1, n3, nr), F32),
         pltpu.VMEM((8, 8), F32),
         pltpu.SMEM((16,), F32),
         pltpu.SMEM((2, 16), F32),
@@ -757,8 +764,8 @@
         pltpu.VMEM((256, 256), BF16),
         pltpu.VMEM((256, 256), BF16),
         pltpu.VMEM((256 * 8, LANES), F32),
-        pltpu.VMEM((8, LANES), F32),
-        pltpu.VMEM((3, 8, 8, LANES), F32),
+        pltpu.VMEM((2, 8, LANES), F32),
+        pltpu.VMEM((3, 8, 2, LANES), F32),
         dma((17,)),
         dma((n2, 8)),
         dma((n2, 8)),
@@ -772,8 +779,8 @@
         dma((2, n2)),
         dma((2, n2)),
         dma((2, n2)),
-        dma((4,)),
-        dma((4,)),
+        dma((2 * n2,)),
+        dma((2 * n2,)),
         dma((3, 8)),
         dma((3, 8)),
         dma((n2,)),

time: 87.1 us -> 83.4 us (0.958)
  the two profiles are of different devices: /device:TPU:2 before, /device:TPU:1 now
where the time goes in v5:
time: 83.4 us; the launch traced here: 82.8 us
  Pallas kernels  82.1 us (98%)
    pallas_call x1, Pallas kernels, shards(): pl.pallas_call(kernel, out_shape=(jax.ShapeDtypeStruct(block, F32), jax.S...  79.1 us
    pallas_call x1, Pallas kernels, shards(): pl.pallas_call(finish, out_shape=(jax.ShapeDtypeStruct(vectors.shape, F32...  2.98 us

profile of v5, /device:TPU:1, one launch (start us, length us, event | category | flops | bytes accessed | tf_op | source)
XLA Modules:
  0.0 82.8 jit_solution(5734892566966162502)
XLA Ops:
  0.6 79.1 %lanczos.1 = (f32[8,2,4,8,512]{4,3,2,1,0:T(8,128)}, f32[3,8,128]{2,1,0:T(8,128)}) custom-call(f32[1,8,2,4,8,512]{5,4,3,2,1,0:T(8,128)} %vec.3, f32[1,8,2,4,8,512]{5,4,3,2,1,0:T(8,128)} %prev.1, f32[2,4,8,512]{3,2,1,0:T(8,128)} %pot.1, f32[2,4,8,512]{3,2,1,0:T(8,128)} %cor.1, f32[2,4,8,512]{3,2,1,0:T(8,128)} %sec.1, f32[8,8]{1,0:T(8,128)} %beta_hbm.1, ...), custom_call_target="tpu_custom_call" | custom-call | tf_op jit(solution)/shard_map/lanczos/pallas_call | solution.py:788
  79.8 3.0 %basis.1 = (f32[1,8,2,4,8,512]{5,4,3,2,1,0:T(8,128)}, f32[8,8]{1,0:T(8,128)}, f32[8,8]{1,0:T(8,128)}) custom-call(f32[1,8,2,4,8,512]{5,4,3,2,1,0:T(8,128)} %vec.3, f32[8,2,4,8,512]{4,3,2,1,0:T(8,128)} %get-tuple-element.5.wfin, f32[3,8,128]{2,1,0:T(8,128)} %get-tuple-element.6.pack_hbm), custom_call_target="tpu_custom_call" | custom-call | tf_op jit(solution)/shard_map/basis/pallas_call | solution.py:802

commit v6 on v5

--- a/solution.py
+++ b/solution.py
@@ -137,6 +137,8 @@
     ars,
     arr,
     obs,
+    zc,
+    yc,
 ):
     ka = lax.axis_index("ka")
     z = lax.axis_index("mode")
@@ -289,32 +291,42 @@
     barrier = pltpu.get_barrier_semaphore()
     edge = jnp.logical_or(ka == 7, ka == 8)
 
-    for i in range(1, 8):
-        for peer in (z_peer, y_peer, x_peer):
-            pl.semaphore_signal(barrier, inc=1, device_id=peer(far_first(i)))
+    for o in range(1, 8):
+        pl.semaphore_signal(barrier, inc=1, device_id=x_peer(o))
+    for o in (1, 7):
+        pl.semaphore_signal(barrier, inc=1, device_id=y_peer(o))
+        pl.semaphore_signal(barrier, inc=1, device_id=z_peer(o))
 
     @pl.when(edge)
     def _():
         pl.semaphore_signal(barrier, inc=1, device_id={"ka": 15 - ka})
 
-    pl.semaphore_wait(barrier, 21 + edge.astype(jnp.int32))
-
-    def start_chunk(c):
-        @pl.loop(1, 8)
-        def _(o):
-            z_forward(c, far_first(o)).start()
-
-        for d in range(2):
-
-            send_on(0, c, d, can_send[d])
+    pl.semaphore_wait(barrier, 11 + edge.astype(jnp.int32))
+
+    def farther(sem, peer):
+        pl.semaphore_signal(sem.at[0], inc=1, device_id=peer(1))
+        pl.semaphore_signal(sem.at[1], inc=1, device_id=peer(7))
+        pl.semaphore_wait(sem.at[0], 1)
+        pl.semaphore_wait(sem.at[1], 1)
+
+    def z_sends(offsets):
+        for c in range(n2):
+            for o in offsets:
+                z_forward(c, o).start()
 
     for o in range(1, 4):
         r_forward(o).start()
-    start_chunk(0)
+    z_sends((1, 7))
+    for c in range(n2):
+        for d in range(2):
+            send_on(0, c, d, can_send[d])
+    for offsets in ((2, 6), (3, 5), (4,)):
+        farther(zc, z_peer)
+        z_sends(offsets)
     for copy in small + locals_:
         copy.start()
-    for c in range(1, n2):
-        start_chunk(c)
+    for _ in range(3):
+        farther(yc, y_peer)
 
     for d in range(2):
 
@@ -663,7 +675,7 @@
         ar_copy(2, i).wait_send()
 
 
-def finish(vec, wfin, pack_hbm, out, alpha_hbm, lower_hbm, v, w, ob, pack, coef, small, sem):
+def finish(vec, wfin, pack_hbm, out, alpha_hbm, lower_hbm, v, w, ob, pack, coef, small, sem, osem):
     n2 = v.shape[2]
 
     def loads(c):
@@ -691,8 +703,9 @@
         coef[j * 8 : j * 8 + 8, :] = col(work, 8 + j)
         coef[64 + j * 8 : 72 + j * 8, :] = -col(work, 16 + j)
 
-    def out_copy(c):
-        return pltpu.make_async_copy(ob.at[:, :, c], out.at[0, :, :, c], sem.at[2, c])
+    def out_copy(k):
+        m, c = k % 2, k // 2
+        return pltpu.make_async_copy(ob.at[:, m, c], out.at[0, :, m, c], osem.at[k])
 
     @pl.loop(0, n2)
     def _(c):
@@ -715,11 +728,14 @@
                 for q in range(2):
                     ob[i, m, c, :, at[q]] = total[q]
 
-        out_copy(c).start()
-
-    @pl.loop(0, n2)
-    def _(c):
-        out_copy(c).wait()
+            @pl.when(h == 1)
+            def _():
+                out_copy(2 * c + m).start()
+
+
+    @pl.loop(0, 2 * n2)
+    def _(k):
+        out_copy(k).wait()
 
     for copy in tiny:
         copy.wait()
@@ -784,6 +800,8 @@
         dma((3, 8)),
         dma((3, 8)),
         dma((n2,)),
+        pltpu.SemaphoreType.REGULAR((2,)),
+        pltpu.SemaphoreType.REGULAR((2,)),
     ]
     wfin, pack = pl.pallas_call(
         kernel,
@@ -816,6 +834,7 @@
             pltpu.VMEM((128, LANES), F32),
             pltpu.VMEM((2, nv, nv), F32),
             dma((4, n2)),
+            dma((2 * n2,)),
         ],
         compiler_params=pltpu.CompilerParams(vmem_limit_bytes=67043328),
         name="basis",

time: 83.4 us -> 86.6 us (1.038)
  Pallas kernels: 82.1 us -> 84.9 us
    pallas_call x1, Pallas kernels: 79.1 us -> 81.9 us  [shards(): pl.pallas_call(kernel, out_shape=(jax.ShapeDtypeStruct(block, F32), jax.S...]
where the time goes in v6:
time: 86.6 us; the launch traced here: 85.5 us
  Pallas kernels  84.9 us (98%)
    pallas_call x1, Pallas kernels, shards(): pl.pallas_call(kernel, out_shape=(jax.ShapeDtypeStruct(block, F32), jax.S...  81.9 us
    pallas_call x1, Pallas kernels, shards(): pl.pallas_call(finish, out_shape=(jax.ShapeDtypeStruct(vectors.shape, F32...  3.01 us

profile of v6, /device:TPU:1, one launch (start us, length us, event | category | flops | bytes accessed | tf_op | source)
XLA Modules:
  0.0 85.5 jit_solution(15941216560301315976)
XLA Ops:
  0.6 81.9 %lanczos.1 = (f32[8,2,4,8,512]{4,3,2,1,0:T(8,128)}, f32[3,8,128]{2,1,0:T(8,128)}) custom-call(f32[1,8,2,4,8,512]{5,4,3,2,1,0:T(8,128)} %vec.3, f32[1,8,2,4,8,512]{5,4,3,2,1,0:T(8,128)} %prev.1, f32[2,4,8,512]{3,2,1,0:T(8,128)} %pot.1, f32[2,4,8,512]{3,2,1,0:T(8,128)} %cor.1, f32[2,4,8,512]{3,2,1,0:T(8,128)} %sec.1, f32[8,8]{1,0:T(8,128)} %beta_hbm.1, ...), custom_call_target="tpu_custom_call" | custom-call | tf_op jit(solution)/shard_map/lanczos/pallas_call | solution.py:806
  82.5 3.0 %basis.1 = (f32[1,8,2,4,8,512]{5,4,3,2,1,0:T(8,128)}, f32[8,8]{1,0:T(8,128)}, f32[8,8]{1,0:T(8,128)}) custom-call(f32[1,8,2,4,8,512]{5,4,3,2,1,0:T(8,128)} %vec.3, f32[8,2,4,8,512]{4,3,2,1,0:T(8,128)} %get-tuple-element.5.wfin, f32[3,8,128]{2,1,0:T(8,128)} %get-tuple-element.6.pack_hbm), custom_call_target="tpu_custom_call" | custom-call | tf_op jit(solution)/shard_map/basis/pallas_call | solution.py:820

commit v7 on v6

--- a/solution.py
+++ b/solution.py
@@ -309,20 +309,23 @@
         pl.semaphore_wait(sem.at[0], 1)
         pl.semaphore_wait(sem.at[1], 1)
 
-    def z_sends(offsets):
-        for c in range(n2):
-            for o in offsets:
-                z_forward(c, o).start()
-
     for o in range(1, 4):
         r_forward(o).start()
-    z_sends((1, 7))
+    for o in (1, 7):
+        z_forward(0, o).start()
     for c in range(n2):
         for d in range(2):
             send_on(0, c, d, can_send[d])
     for offsets in ((2, 6), (3, 5), (4,)):
         farther(zc, z_peer)
-        z_sends(offsets)
+        for o in offsets:
+            z_forward(0, o).start()
+    for c in range(1, n2):
+
+        @pl.loop(1, 8)
+        def _(i):
+            z_forward(c, far_first(i)).start()
+
     for copy in small + locals_:
         copy.start()
     for _ in range(3):
@@ -492,6 +495,15 @@
 
     @pl.loop(0, n2)
     def _(c):
+        for d in range(2):
+            wait_recv_when(has_one[d], y_own(c, d))
+
+            send_on(1, c, d, jnp.logical_and(has_one[d], can_send[d]))
+
+        @pl.when(c < VIA)
+        def _():
+            pass_on(0, c)
+
         @pl.loop(1, 8)
         def _(o):
             z_forward(c, o).wait_recv()
@@ -501,15 +513,6 @@
         @pl.loop(1, 8)
         def _(o):
             z_back(c, far_first(o)).start()
-
-        for d in range(2):
-            wait_recv_when(has_one[d], y_own(c, d))
-
-            send_on(1, c, d, jnp.logical_and(has_one[d], can_send[d]))
-
-        @pl.when(c < VIA)
-        def _():
-            pass_on(0, c)
 
         @pl.when(c == 1)
         def _():

time: 86.6 us -> 83.5 us (0.964)
  Pallas kernels: 84.9 us -> 82.4 us
    pallas_call x1, Pallas kernels: 81.9 us -> 79.4 us  [shards(): pl.pallas_call(kernel, out_shape=(jax.ShapeDtypeStruct(block, F32), jax.S...]
where the time goes in v7:
time: 83.5 us; the launch traced here: 83.1 us
  Pallas kernels  82.4 us (99%)
    pallas_call x1, Pallas kernels, shards(): pl.pallas_call(kernel, out_shape=(jax.ShapeDtypeStruct(block, F32), jax.S...  79.4 us
    pallas_call x1, Pallas kernels, shards(): pl.pallas_call(finish, out_shape=(jax.ShapeDtypeStruct(vectors.shape, F32...  3.01 us

profile of v7, /device:TPU:1, one launch (start us, length us, event | category | flops | bytes accessed | tf_op | source)
XLA Modules:
  0.0 83.1 jit_solution(16431933519583541938)
XLA Ops:
  0.6 79.4 %lanczos.1 = (f32[8,2,4,8,512]{4,3,2,1,0:T(8,128)}, f32[3,8,128]{2,1,0:T(8,128)}) custom-call(f32[1,8,2,4,8,512]{5,4,3,2,1,0:T(8,128)} %vec.3, f32[1,8,2,4,8,512]{5,4,3,2,1,0:T(8,128)} %prev.1, f32[2,4,8,512]{3,2,1,0:T(8,128)} %pot.1, f32[2,4,8,512]{3,2,1,0:T(8,128)} %cor.1, f32[2,4,8,512]{3,2,1,0:T(8,128)} %sec.1, f32[8,8]{1,0:T(8,128)} %beta_hbm.1, ...), custom_call_target="tpu_custom_call" | custom-call | tf_op jit(solution)/shard_map/lanczos/pallas_call | solution.py:809
  80.1 3.0 %basis.1 = (f32[1,8,2,4,8,512]{5,4,3,2,1,0:T(8,128)}, f32[8,8]{1,0:T(8,128)}, f32[8,8]{1,0:T(8,128)}) custom-call(f32[1,8,2,4,8,512]{5,4,3,2,1,0:T(8,128)} %vec.3, f32[8,2,4,8,512]{4,3,2,1,0:T(8,128)} %get-tuple-element.5.wfin, f32[3,8,128]{2,1,0:T(8,128)} %get-tuple-element.6.pack_hbm), custom_call_target="tpu_custom_call" | custom-call | tf_op jit(solution)/shard_map/basis/pallas_call | solution.py:823

commit v8 on v5

--- a/solution.py
+++ b/solution.py
@@ -480,6 +480,15 @@
 
     @pl.loop(0, n2)
     def _(c):
+        for d in range(2):
+            wait_recv_when(has_one[d], y_own(c, d))
+
+            send_on(1, c, d, jnp.logical_and(has_one[d], can_send[d]))
+
+        @pl.when(c < VIA)
+        def _():
+            pass_on(0, c)
+
         @pl.loop(1, 8)
         def _(o):
             z_forward(c, o).wait_recv()
@@ -489,15 +498,6 @@
         @pl.loop(1, 8)
         def _(o):
             z_back(c, far_first(o)).start()
-
-        for d in range(2):
-            wait_recv_when(has_one[d], y_own(c, d))
-
-            send_on(1, c, d, jnp.logical_and(has_one[d], can_send[d]))
-
-        @pl.when(c < VIA)
-        def _():
-            pass_on(0, c)
 
         @pl.when(c == 1)
         def _():
@@ -635,7 +635,15 @@
         return total
 
     own = [jnp.where(lane % 8 == row, msg[a : a + 1, :], 0.0) for a in range(2)]
-    whole = exact(jnp.concatenate(own, axis=0), hot((LANES, LANES), lambda q: q // 8))
+    own = jnp.concatenate(own, axis=0)
+    high, low = halves(own)
+    rest = ((own - high.astype(F32)) - low.astype(F32)).astype(BF16)
+    parts = jnp.dot(
+        jnp.concatenate([high, low, rest], axis=0),
+        hot((LANES, LANES), lambda q: q // 8).astype(BF16),
+        preferred_element_type=F32,
+    )
+    whole = parts[0:16] + (parts[16:32] + parts[32:48])
     overlap = whole[0:8]
     first_t = pltpu.roll(overlap, LANES - 8, axis=1)
     square = whole[8:16]
@@ -653,7 +661,7 @@
         column = col(work, k)
         root = lax.rsqrt(pivot)
         factor = jnp.where((lane == k) & (row >= k), column * root, factor)
-        below = work - (column / pivot) * prow
+        below = work - (column * (root * root)) * prow
         work = jnp.where(row > k, below, jnp.where(row == k, work * root, work))
     pack[0] = work
     pack[1] = both

time: 83.4 us -> 83.1 us (level)
  no operation moved by 1% of the time
where the time goes in v8:
time: 83.1 us; the launch traced here: 82.6 us
  Pallas kernels  82 us (99%)
    pallas_call x1, Pallas kernels, shards(): pl.pallas_call(kernel, out_shape=(jax.ShapeDtypeStruct(block, F32), jax.S...  79 us
    pallas_call x1, Pallas kernels, shards(): pl.pallas_call(finish, out_shape=(jax.ShapeDtypeStruct(vectors.shape, F32...  2.98 us

profile of v8, /device:TPU:1, one launch (start us, length us, event | category | flops | bytes accessed | tf_op | source)
XLA Modules:
  0.0 82.6 jit_solution(10734407233527754521)
XLA Ops:
  0.6 79.0 %lanczos.1 = (f32[8,2,4,8,512]{4,3,2,1,0:T(8,128)}, f32[3,8,128]{2,1,0:T(8,128)}) custom-call(f32[1,8,2,4,8,512]{5,4,3,2,1,0:T(8,128)} %vec.3, f32[1,8,2,4,8,512]{5,4,3,2,1,0:T(8,128)} %prev.1, f32[2,4,8,512]{3,2,1,0:T(8,128)} %pot.1, f32[2,4,8,512]{3,2,1,0:T(8,128)} %cor.1, f32[2,4,8,512]{3,2,1,0:T(8,128)} %sec.1, f32[8,8]{1,0:T(8,128)} %beta_hbm.1, ...), custom_call_target="tpu_custom_call" | custom-call | tf_op jit(solution)/shard_map/lanczos/pallas_call | solution.py:796
  79.6 3.0 %basis.1 = (f32[1,8,2,4,8,512]{5,4,3,2,1,0:T(8,128)}, f32[8,8]{1,0:T(8,128)}, f32[8,8]{1,0:T(8,128)}) custom-call(f32[1,8,2,4,8,512]{5,4,3,2,1,0:T(8,128)} %vec.3, f32[8,2,4,8,512]{4,3,2,1,0:T(8,128)} %get-tuple-element.5.wfin, f32[3,8,128]{2,1,0:T(8,128)} %get-tuple-element.6.pack_hbm), custom_call_target="tpu_custom_call" | custom-call | tf_op jit(solution)/shard_map/basis/pallas_call | solution.py:810

commit v9 on v8

--- a/solution.py
+++ b/solution.py
@@ -420,7 +420,7 @@
 
         rret[pl.ds(2 * r, 2)] = rout[r]
 
-    def gather_products(c, left, right, spots, triangle):
+    def gather_products(c, left, right, spot_of, triangle):
         for g in range(4):
             pairs = [(j, i) for i in (2 * g, 2 * g + 1) for j in range(8) if j <= i or not triangle]
             sums = {}
@@ -432,8 +432,8 @@
                         term = ls[j] * rs[i - 2 * g]
                         sums[j, i] = term if (j, i) not in sums else sums[j, i] + term
             for j, i in pairs:
-                for spot in spots(j, i):
-                    acc[spot * 8 : spot * 8 + 8, :] += sums[j, i]
+                spot = spot_of(j, i)
+                acc[spot * 8 : spot * 8 + 8, :] += sums[j, i]
 
     def local_terms(c):
         x = v[:, :, c].reshape(nv * n1 * 8, 512)
@@ -456,7 +456,7 @@
                         taken = taken + splat(tabb, i * 8 + j) * old[j]
                     w[i, m, c, :, at] = total - taken
 
-        gather_products(c, v, v, lambda j, i: {(24 + j) * 8 + i, (24 + i) * 8 + j}, True)
+        gather_products(c, v, v, lambda j, i: (16 + j) * 8 + i, True)
 
     def turn(x):
         flat = x.reshape(nv * n1 * 8, 512)
@@ -529,7 +529,7 @@
             total[a] = packed
 
     total[...] = jnp.zeros((2, 8, LANES), F32)
-    sum_into(8, 0, 24)
+    sum_into(8, 0, 16)
 
     def w_copy(c):
         return pltpu.make_async_copy(w.at[:, :, c], wout.at[:, :, c], obs.at[c])
@@ -597,10 +597,10 @@
                 w[n, m, c] = (w[n, m, c] + rret[n, m, c]) + (zret[n, m, c] + skip)
 
         w_copy(c).start()
-        gather_products(c, v, w, lambda j, i: (j * 8 + i, (16 + i) * 8 + j), False)
-        gather_products(c, w, w, lambda j, i: {(8 + j) * 8 + i, (8 + i) * 8 + j}, True)
-
-    sum_into(24, 8, 0)
+        gather_products(c, v, w, lambda j, i: j * 8 + i, False)
+        gather_products(c, w, w, lambda j, i: (8 + j) * 8 + i, True)
+
+    sum_into(16, 8, 0)
     msg = jnp.concatenate([jnp.sum(total[a], axis=0, keepdims=True) for a in range(2)], axis=0)
 
     groups = ((u, x_peer), (z, z_peer), (y, y_peer))
@@ -615,9 +615,9 @@
         arb[g, groups[g][0]] = msg
         for i in range(1, 8):
             ar_copy(g, far_first(i)).start()
-        if g == 0:
+        if g == 1:
             wait_sends_back()
-        else:
+        if g > 0:
             for i in range(1, 8):
                 ar_copy(g - 1, i).wait_send()
         for i in range(1, 8):
@@ -634,20 +634,38 @@
             total = total + col(a, k) * b[k : k + 1, :]
         return total
 
-    own = [jnp.where(lane % 8 == row, msg[a : a + 1, :], 0.0) for a in range(2)]
-    own = jnp.concatenate(own, axis=0)
-    high, low = halves(own)
-    rest = ((own - high.astype(F32)) - low.astype(F32)).astype(BF16)
-    parts = jnp.dot(
-        jnp.concatenate([high, low, rest], axis=0),
-        hot((LANES, LANES), lambda q: q // 8).astype(BF16),
-        preferred_element_type=F32,
+    def select(own, column):
+        high, low = halves(own)
+        rest = ((own - high.astype(F32)) - low.astype(F32)).astype(BF16)
+        parts = jnp.dot(
+            jnp.concatenate([high, low, rest], axis=0),
+            hot((LANES, LANES), column).astype(BF16),
+            preferred_element_type=F32,
+        )
+        n = own.shape[0]
+        return parts[0:n] + (parts[n : 2 * n] + parts[2 * n : 3 * n])
+
+    rows_of = [msg[a : a + 1, :] for a in range(2)]
+    within, block = lane % 8, lane // 8
+    plain = select(
+        jnp.concatenate([jnp.where(within == row, x, 0.0) for x in rows_of], axis=0),
+        lambda q: q // 8,
     )
-    whole = parts[0:16] + (parts[16:32] + parts[32:48])
-    overlap = whole[0:8]
-    first_t = pltpu.roll(overlap, LANES - 8, axis=1)
-    square = whole[8:16]
-    first = pltpu.roll(square, LANES - 8, axis=1)
+    turned_over = select(
+        jnp.concatenate(
+            [
+                jnp.where(block == row, rows_of[0], 0.0),
+                jnp.where(block == row + 8, rows_of[0], 0.0),
+                jnp.where(block == row, rows_of[1], 0.0),
+            ],
+            axis=0,
+        ),
+        lambda q: q % 8,
+    )
+    first_t = pltpu.roll(plain[0:8], LANES - 8, axis=1)
+    first = turned_over[8:16]
+    overlap = jnp.where(lane <= row, plain[0:8], turned_over[0:8])
+    square = jnp.where(lane <= row, plain[8:16], turned_over[16:24])
     both_t = 2.0 * first_t - mm(first_t, overlap)
     both = 2.0 * first - mm(overlap, first)
     gram = square - mm(both_t, first) - mm(first_t, both) + mm(mm(both_t, overlap), both)
@@ -771,7 +789,7 @@
         pltpu.VMEM((nr, nr), BF16),
         pltpu.VMEM((256, 256), BF16),
         pltpu.VMEM((256, 256), BF16),
-        pltpu.VMEM((256 * 8, LANES), F32),
+        pltpu.VMEM((192 * 8, LANES), F32),
         pltpu.VMEM((2, 8, LANES), F32),
         pltpu.VMEM((3, 8, 2, LANES), F32),
         dma((17,)),

time: 83.1 us -> 83 us (level)
  no operation moved by 1% of the time
where the time goes in v9:
time: 83 us; the launch traced here: 82.6 us
  Pallas kernels  81.9 us (99%)
    pallas_call x1, Pallas kernels, shards(): pl.pallas_call(kernel, out_shape=(jax.ShapeDtypeStruct(block, F32), jax.S...  78.9 us
    pallas_call x1, Pallas kernels, shards(): pl.pallas_call(finish, out_shape=(jax.ShapeDtypeStruct(vectors.shape, F32...  2.98 us

profile of v9, /device:TPU:1, one launch (start us, length us, event | category | flops | bytes accessed | tf_op | source)
XLA Modules:
  0.0 82.6 jit_solution(14538878176241449829)
XLA Ops:
  0.6 78.9 %lanczos.1 = (f32[8,2,4,8,512]{4,3,2,1,0:T(8,128)}, f32[3,8,128]{2,1,0:T(8,128)}) custom-call(f32[1,8,2,4,8,512]{5,4,3,2,1,0:T(8,128)} %vec.3, f32[1,8,2,4,8,512]{5,4,3,2,1,0:T(8,128)} %prev.1, f32[2,4,8,512]{3,2,1,0:T(8,128)} %pot.1, f32[2,4,8,512]{3,2,1,0:T(8,128)} %cor.1, f32[2,4,8,512]{3,2,1,0:T(8,128)} %sec.1, f32[8,8]{1,0:T(8,128)} %beta_hbm.1, ...), custom_call_target="tpu_custom_call" | custom-call | tf_op jit(solution)/shard_map/lanczos/pallas_call | solution.py:814
  79.6 3.0 %basis.1 = (f32[1,8,2,4,8,512]{5,4,3,2,1,0:T(8,128)}, f32[8,8]{1,0:T(8,128)}, f32[8,8]{1,0:T(8,128)}) custom-call(f32[1,8,2,4,8,512]{5,4,3,2,1,0:T(8,128)} %vec.3, f32[8,2,4,8,512]{4,3,2,1,0:T(8,128)} %get-tuple-element.5.wfin, f32[3,8,128]{2,1,0:T(8,128)} %get-tuple-element.6.pack_hbm), custom_call_target="tpu_custom_call" | custom-call | tf_op jit(solution)/shard_map/basis/pallas_call | solution.py:828

commit v10 on v9

--- a/solution.py
+++ b/solution.py
@@ -310,7 +310,10 @@
 
     for o in range(1, 4):
         r_forward(o).start()
-    start_chunk(0)
+    for d in range(2):
+        send_on(0, 0, d, can_send[d])
+    for i in range(1, 8):
+        z_forward(0, far_first(i)).start()
     for copy in small + locals_:
         copy.start()
     for c in range(1, n2):

time: 83 us -> 83 us (level)
  no operation moved by 1% of the time
where the time goes in v10:
time: 83 us; the launch traced here: 82.6 us
  Pallas kernels  82 us (99%)
    pallas_call x1, Pallas kernels, shards(): pl.pallas_call(kernel, out_shape=(jax.ShapeDtypeStruct(block, F32), jax.S...  79 us
    pallas_call x1, Pallas kernels, shards(): pl.pallas_call(finish, out_shape=(jax.ShapeDtypeStruct(vectors.shape, F32...  2.98 us

profile of v10, /device:TPU:1, one launch (start us, length us, event | category | flops | bytes accessed | tf_op | source)
XLA Modules:
  0.0 82.6 jit_solution(17001391428871851627)
XLA Ops:
  0.6 79.0 %lanczos.1 = (f32[8,2,4,8,512]{4,3,2,1,0:T(8,128)}, f32[3,8,128]{2,1,0:T(8,128)}) custom-call(f32[1,8,2,4,8,512]{5,4,3,2,1,0:T(8,128)} %vec.3, f32[1,8,2,4,8,512]{5,4,3,2,1,0:T(8,128)} %prev.1, f32[2,4,8,512]{3,2,1,0:T(8,128)} %pot.1, f32[2,4,8,512]{3,2,1,0:T(8,128)} %cor.1, f32[2,4,8,512]{3,2,1,0:T(8,128)} %sec.1, f32[8,8]{1,0:T(8,128)} %beta_hbm.1, ...), custom_call_target="tpu_custom_call" | custom-call | tf_op jit(solution)/shard_map/lanczos/pallas_call | solution.py:817
  79.7 3.0 %basis.1 = (f32[1,8,2,4,8,512]{5,4,3,2,1,0:T(8,128)}, f32[8,8]{1,0:T(8,128)}, f32[8,8]{1,0:T(8,128)}) custom-call(f32[1,8,2,4,8,512]{5,4,3,2,1,0:T(8,128)} %vec.3, f32[8,2,4,8,512]{4,3,2,1,0:T(8,128)} %get-tuple-element.5.wfin, f32[3,8,128]{2,1,0:T(8,128)} %get-tuple-element.6.pack_hbm), custom_call_target="tpu_custom_call" | custom-call | tf_op jit(solution)/shard_map/basis/pallas_call | solution.py:831
